TPU v7x, 32 devices: a whole 2x2x4 slice. The times are simulated.
32 devices in a mesh: dp: 8 (over z, x), tensor: 4 (over y, core).
Axes of the slice: x: 2, y: 2, z: 4, core: 2. Of those that a mesh axis runs over, the one named last changes fastest.
Arguments:
- tokens: bfloat16 [16, 512, 768], P('dp'), may hold values from -6 to 6
- lengths: int32 [16], P('dp'), may hold values from 1 to 512, 2048 in all
- groups: int32 [16, 512], P('dp'), may hold values from 0 to 3, never falling along the last dimension, each value on 1 to 256 neighbouring positions
- key_mask: int32 [16, 512], P('dp'), may hold values 0 or 1
- w_query: bfloat16 [768, 768], P(None, 'tensor'), may hold values from -0.21875 to 0.21875
- b_query: float32 [768], P('tensor'), may hold values from -3 to 3
- w_key: bfloat16 [768, 768], P(None, 'tensor'), may hold values from -0.21875 to 0.21875
- w_value: bfloat16 [768, 768], P(None, 'tensor'), may hold values from -0.21875 to 0.21875
- b_value: float32 [768], P('tensor'), may hold values from -3 to 3
- rel_bias: float32 [12, 256], P('tensor'), may hold values from -4 to 4
- w_out: bfloat16 [768, 768], P('tensor'), may hold values from -0.625 to 0.625
- b_out: float32 [768], replicated, may hold values from -3 to 3
- gain_one: float32 [768], replicated, may hold values from 0.25 to 1.75
- shift_one: float32 [768], replicated, may hold values from -3 to 3
- w_inner: bfloat16 [768, 3072], P(None, 'tensor'), may hold values from -0.21875 to 0.21875
- b_inner: float32 [3072], P('tensor'), may hold values from -3 to 3
- w_outer: bfloat16 [3072, 768], P('tensor'), may hold values from -0.109375 to 0.109375
- b_outer: float32 [768], replicated, may hold values from -3 to 3
- gain_two: float32 [768], replicated, may hold values from 0.25 to 1.75
- shift_two: float32 [768], replicated, may hold values from -3 to 3
- cotangent: bfloat16 [16, 256, 768], P('dp'), may hold values from -24 to 24
Outputs:
- output: bfloat16 [16, 256, 768], P('dp')
- grad_tokens: bfloat16 [16, 512, 768], P('dp')
- grad_w_query: float32 [768, 768], P(None, 'tensor')
- grad_b_query: float32 [768], P('tensor')
- grad_w_key: float32 [768, 768], P(None, 'tensor')
- grad_w_value: float32 [768, 768], P(None, 'tensor')
- grad_b_value: float32 [768], P('tensor')
- grad_rel_bias: float32 [12, 256], P('tensor')
- grad_w_out: float32 [768, 768], P('tensor')
- grad_b_out: float32 [768], replicated
- grad_gain_one: float32 [768], replicated
- grad_shift_one: float32 [768], replicated
- grad_w_inner: float32 [768, 3072], P(None, 'tensor')
- grad_b_inner: float32 [3072], P('tensor')
- grad_w_outer: float32 [3072, 768], P('tensor')
- grad_b_outer: float32 [768], replicated
- grad_gain_two: float32 [768], replicated
- grad_shift_two: float32 [768], replicated
Inputs may be any that keep to these rules, and one draw needn't show every extreme that they name: `lengths`: the longest row has exactly 512 used tokens. `groups`: document ids never fall along a row; a document has at most half of 512 positions.
All inputs are finite; a program needn't handle non-finite values. No bound on the sum of `lengths` or of `key_mask` on one device may be relied on, other than what follows from the above.
Results may differ from a plain program's by a relative error of at most 0.013.
Values sent between devices are 32-bit elements; how exact they have to be, the bound alone decides.
No kernel may reach another device: no remote copies, remote signals or barrier semaphores. Data moves between devices by JAX's collectives and lax.ppermute only.
A program may use at most 128 MiB of HBM per device.

v0:
```python
import functools

import jax
import jax.numpy as jnp
from jax import lax
from jax.experimental import pallas as pl
from jax.experimental.pallas import tpu as pltpu
from jax.sharding import PartitionSpec as P

F32 = jnp.float32
BF16 = jnp.bfloat16
VMEM_BYTES = 12 << 20
PIECE = 32

INWARD = [(0, 2), (1, 3), (6, 4), (7, 5)]
MIDDLE = [(2, 4), (3, 5), (4, 2), (5, 3)]
OUTWARD = [(2, 0), (3, 1), (4, 6), (5, 7)]
CENTRE_X = [(2, 3), (3, 2), (4, 5), (5, 4)]


def swap_pairs(n, bit):
    return [(i, i ^ bit) for i in range(n)]


def core_swap(a):
    return lax.ppermute(a, "tensor", swap_pairs(lax.axis_size("tensor"), 1))


def chip_swap(a):
    return lax.ppermute(a, "tensor", swap_pairs(lax.axis_size("tensor"), 2))


def x_swap(a):
    return lax.ppermute(a, "dp", swap_pairs(lax.axis_size("dp"), 1))


def hop(a, pairs):
    return lax.ppermute(a, "dp", pairs)


def on_line_of_four():
    return lax.axis_size("dp") == 8


def core_bit():
    return lax.axis_index("tensor") & 1


def x_bit():
    return lax.axis_index("dp") & 1


def centre_half():
    return ((lax.axis_index("dp") >> 1) >= 2).astype(jnp.int32)


def in_centre():
    z = lax.axis_index("dp") >> 1
    return (z == 1) | (z == 2)


def nn(a, b):
    return jnp.dot(a, b, preferred_element_type=F32)


def nt(a, b):
    return lax.dot_general(a, b, (((1,), (1,)), ((), ())), preferred_element_type=F32)


def tn(a, b):
    return lax.dot_general(a, b, (((0,), (0,)), ((), ())), preferred_element_type=F32)


def shape(dims, dtype=F32):
    return jax.ShapeDtypeStruct(dims, dtype)


ANY = pl.BlockSpec(memory_space=pl.ANY)
VMEM = pl.BlockSpec(memory_space=pltpu.VMEM)


class View:
    def __init__(self, ref, pick):
        self.ref = ref if pick is None else ref.at[pick]
        self.shape = self.ref.shape

    def __getitem__(self, at):
        value = self.ref[at]
        return value.reshape(1, -1) if len(self.shape) == 1 and at is Ellipsis else value


def begin(token):
    token[...] = jnp.zeros_like(token)


class Line:
    def __init__(self):
        self.token = pl.pallas_call(
            begin,
            out_specs=VMEM,
            out_shape=shape((8, 128)),
            cost_estimate=pl.CostEstimate(flops=1 << 31, bytes_accessed=1 << 20, transcendentals=0),
        )()

    def __call__(self, body, outs, ins, late=(), scratch=(), left=(), onto=()):
        late = [item if isinstance(item, tuple) else (item, None) for item in late]
        far, near, given = len(late), len(ins), len(outs)

        def kernel(*refs):
            views = [View(ref, pick) for ref, (_, pick) in zip(refs, late, strict=False)]
            rest = refs[far + near + 1 :]
            body(*views, *refs[far : far + near], *rest[:given], *rest[given + 1 :])

        result = pl.pallas_call(
            kernel,
            name=getattr(body, "func", body).__name__,
            in_specs=[VMEM] * far
            + [ANY if i in onto else VMEM for i in range(near)]
            + [ANY],
            out_specs=[ANY if i in left else VMEM for i in range(given)] + [ANY],
            out_shape=[*outs, shape(self.token.shape)],
            scratch_shapes=list(scratch),
            input_output_aliases={far + i: o for i, o in zip(onto, left, strict=False)},
            compiler_params=pltpu.CompilerParams(vmem_limit_bytes=VMEM_BYTES),
            cost_estimate=pl.CostEstimate(flops=1024, bytes_accessed=1024, transcendentals=0),
        )(*(a for a, _ in late), *ins, self.token)
        self.token = result[-1]
        return result[:-1]


def hand_out(value, keep, send):
    size = keep.shape[0]
    for core in range(2):

        @pl.when(core_bit() == core)
        def _(core=core):
            keep[...] = value[core * size : (core + 1) * size]
            at = (1 - core) * size
            for ref in send:
                ref[...] = value[at : at + ref.shape[0]]
                at += ref.shape[0]


def chip_sum(keep, *refs):
    *got, out = refs
    size = got[0].shape[0]
    for i, ref in enumerate(got):
        at = slice(i * size, (i + 1) * size)
        out[at, :] = keep[at, :] + ref[...]


def total_sum(chip, far, *outs):
    size = outs[0].shape[0]
    for i, ref in enumerate(outs):
        at = slice(i * size, (i + 1) * size)
        ref[...] = chip[at, :] + far[at, :]


def gathered(parts, place):
    size, piece = place.shape[0] // 2, parts[0].shape[0]
    core = core_bit()
    for side, own in ((core, parts[: len(parts) // 2]), (1 - core, parts[len(parts) // 2 :])):
        for i, ref in enumerate(own):
            place[pl.ds(pl.multiple_of(side * size + i * piece, piece), piece), :] = ref[...]
    return place[...]


def head_lanes(size, heads, dim, h):
    lane = lax.broadcasted_iota(jnp.int32, (size, heads * dim), 1)
    return (lane >= h * dim) & (lane < (h + 1) * dim)


def attend(row, lens, tokens, groups, key_mask, wq, bq, wk, wv, bv, rel, wo, ctx, qo, ko, vo, prob, pooled_out, keep, *send):
    heads, table = rel.shape
    seq = tokens.shape[0]
    half = seq // 2
    dim = wq.shape[0] // heads
    tok = tokens[...]
    i = lax.broadcasted_iota(jnp.int32, (half, seq), 0)
    j = lax.broadcasted_iota(jnp.int32, (half, seq), 1)
    pick = jnp.where((j >> 1) == i, 0.5, 0.0).astype(BF16)
    pooled = nn(pick, tok)
    pooled_out[...] = pooled
    q = (nt(pooled.astype(BF16), wq[...]) + bq[...]).astype(BF16)
    k = nt(tok, wk[...]).astype(BF16)
    v = (nt(tok, wv[...]) + bv[...]).astype(BF16)
    qo[...] = q
    ko[...] = k
    vo[...] = v
    self_key = j == 2 * i
    group = groups[row : row + 1, :].astype(F32)
    place = lax.broadcasted_iota(jnp.int32, (1, seq), 1)
    live = (place < lens[...][:, row : row + 1]) & (key_mask[row : row + 1, :] == 1)
    own = jnp.sum(jnp.where(self_key, group, 0.0), axis=1, keepdims=True)
    allowed = self_key | (own == jnp.where(live, group, -1.0))
    out = jnp.zeros((half, heads * dim), F32)
    for h in range(heads):
        span = 2 * seq
        wing = (span - table) // 2
        low = rel[h : h + 1, : table // 2]
        high = rel[h : h + 1, table // 2 :]
        line = jnp.concatenate(
            [
                high,
                jnp.broadcast_to(rel[h : h + 1, table - 1 :], (1, wing)),
                jnp.broadcast_to(rel[h : h + 1, :1], (1, wing)),
                low,
            ],
            axis=1,
        )
        bias = pltpu.roll(jnp.broadcast_to(line, (half, span)), 0, 1, stride=2, stride_axis=0)[:, :seq]
        raw = nt(jnp.where(head_lanes(half, heads, dim, h), q, 0), k) * 0.125 + bias
        score = jnp.where(allowed, raw, -1e30)
        expo = jnp.exp(score - jnp.max(score, axis=1, keepdims=True))
        p = expo * (1.0 / jnp.sum(expo, axis=1, keepdims=True))
        prob[h] = p
        out = out + nn(p.astype(BF16), jnp.where(head_lanes(seq, heads, dim, h), v, 0))
    low_out = out.astype(BF16)
    ctx[...] = low_out
    hand_out(nn(low_out, wo[...]), keep, send)


def normalise(value):
    centre = value - jnp.mean(value, axis=1, keepdims=True)
    factor = lax.rsqrt(jnp.mean(centre * centre, axis=1, keepdims=True) + 1e-05)
    return centre * factor, factor


def forward(count, b_out, gain, shift, wi, bi, wt, pooled, *refs):
    parts, refs = refs[:count], refs[count:]
    normed_o, factor_o, ylow_o, act_o, slope_o, keep, *send, place = refs
    first = pooled[...] + (gathered(parts, place) + b_out[...])
    normed, factor = normalise(first)
    normed_o[...] = normed
    factor_o[...] = factor
    y_low = (normed * gain[...] + shift[...]).astype(BF16)
    ylow_o[...] = y_low
    inner = nn(y_low, wi[...]) + bi[...]
    cdf = 0.5 + 0.5 * lax.erf(inner * 0.7071067811865476)
    slope_o[...] = cdf + inner * (0.3989422804014327 * jnp.exp(-0.5 * inner * inner))
    act = (inner * cdf).astype(BF16)
    act_o[...] = act
    hand_out(nn(act, wt[...]), keep, send)


def norm_back(grad, normed, factor, gain):
    scaled = grad * gain
    one = jnp.mean(scaled, axis=1, keepdims=True)
    two = jnp.mean(scaled * normed, axis=1, keepdims=True)
    return factor * (scaled - one - normed * two)


def over_rows(value):
    return jnp.sum(value, axis=0, keepdims=True)


def turn(row, count, again, gain_one, shift_one, b_outer, gain, shift, cot, wt, wi, normed_one, slope, *refs):
    parts, refs = refs[:count], refs[count + again :]
    result, g_second_o, g_ffn_o, g_inner_o, small, keep, *send, place, low, done = refs
    y_one = normed_one[...] * gain_one[...] + shift_one[...]
    second = y_one + (gathered(parts, place) + b_outer[...])
    normed, factor = normalise(second)
    low[...] = (normed * gain[...] + shift[...]).astype(BF16)
    leave = pltpu.make_async_copy(low, result.at[row], done)
    leave.start()
    g_out = cot[...].astype(F32)
    g_second = norm_back(g_out, normed, factor, gain[...])
    g_second_o[...] = g_second
    g_ffn = g_second.astype(BF16)
    g_ffn_o[...] = g_ffn
    g_inner = (nt(g_ffn, wt[...]) * slope[...]).astype(BF16)
    g_inner_o[...] = g_inner
    hand_out(nt(g_inner, wi[...]), keep, send)
    small[0:1, :] = over_rows(g_inner.astype(F32))
    small[1:2, :] = over_rows(g_second)
    small[2:3, :] = over_rows(g_out * normed)
    small[3:4, :] = over_rows(g_out)
    leave.wait()


def ffn_weights(kind, lo, hi, act0, act1, g_ffn0, g_ffn1, y0, y1, g_in0, g_in1, *outs):
    def block(ref, lhs0, lhs1, rhs0, rhs1):
        ref[...] = tn(lhs0[:, lo:hi], rhs0[...]) + tn(lhs1[:, lo:hi], rhs1[...])

    outer = (act0, act1, g_ffn0, g_ffn1)
    inner = (y0, y1, g_in0, g_in1)
    if kind == "Z":
        block(outs[0].at[0], *outer)
        block(outs[0].at[1], *inner)
        return
    keep, send = outs

    @pl.when(x_bit() == 0)
    def _():
        block(keep, *outer)
        block(send, *inner)

    @pl.when(x_bit() != 0)
    def _():
        block(keep, *inner)
        block(send, *outer)


def attend_back(heads, count, gain, wo, wq, wk, wv, g_second, normed, factor, q_r, k_r, v_r, prob, *refs):
    parts, refs = refs[:count], refs[count:]
    g_first_o, g_attn_o, gs_o, gq_o, gk_o, gv_o, small, keep, *send, place = refs
    g_y = g_second[...] + gathered(parts, place)
    small[0:1, :] = over_rows(g_y * normed[...])
    small[1:2, :] = over_rows(g_y)
    g_first = norm_back(g_y, normed[...], factor[...], gain[...])
    g_first_o[...] = g_first
    small[2:3, :] = over_rows(g_first)
    g_attn = g_first.astype(BF16)
    g_attn_o[...] = g_attn
    g_ctx = nt(g_attn, wo[...]).astype(BF16)
    q, k, v = q_r[...], k_r[...], v_r[...]
    half, seq = q.shape[0], k.shape[0]
    dim = q.shape[1] // heads
    gq = jnp.zeros(q.shape, F32)
    gk = jnp.zeros(k.shape, F32)
    gv = jnp.zeros(k.shape, F32)
    for h in range(heads):
        own_q = head_lanes(half, heads, dim, h)
        own_k = head_lanes(seq, heads, dim, h)
        g_h = jnp.where(own_q, g_ctx, 0)
        p = prob[h]
        g_p = nt(g_h, v)
        g_s = (p * (g_p - jnp.sum(p * g_p, axis=1, keepdims=True))).astype(BF16)
        gs_o[h] = g_s
        gq = gq + nn(g_s, jnp.where(own_k, k, 0))
        gk = gk + tn(g_s, jnp.where(own_q, q, 0))
        gv = gv + tn(p.astype(BF16), g_h)
    gq = (gq * 0.125).astype(BF16)
    gk = (gk * 0.125).astype(BF16)
    gv = gv.astype(BF16)
    gq_o[...] = gq
    gk_o[...] = gk
    gv_o[...] = gv
    i = lax.broadcasted_iota(jnp.int32, (seq, half), 0)
    j = lax.broadcasted_iota(jnp.int32, (seq, half), 1)
    twice = jnp.where((i >> 1) == j, 0.5, 0.0).astype(BF16)
    gq_twice = nn(twice, gq).astype(BF16)
    hand_out(nn(gk, wk[...]) + nn(gv, wv[...]) + nn(gq_twice, wq[...]), keep, send)


def attn_weights_one(tokens, gq0, gq1, gv0, gv1, pooled0, pooled1, keep, send):
    def queries(ref):
        ref[...] = tn(gq0[...], pooled0[...].astype(BF16)) + tn(gq1[...], pooled1[...].astype(BF16))

    def values(ref):
        ref[...] = tn(gv0[...], tokens[0]) + tn(gv1[...], tokens[1])

    @pl.when(x_bit() == 0)
    def _():
        queries(keep)
        values(send)

    @pl.when(x_bit() != 0)
    def _():
        values(keep)
        queries(send)


def attn_weights_two(heads, table, tokens, gq0, gq1, gk0, gk1, gv0, gv1, ctx0, ctx1, ga0, ga1, gs0, gs1, t0, t1, a0, a1, keep, send):
    seq = tokens.shape[1]
    half, e = gq0.shape
    width = tokens.shape[2]
    i = lax.broadcasted_iota(jnp.int32, (half, half), 0)
    j = lax.broadcasted_iota(jnp.int32, (half, half), 1)
    flip = jnp.where(i + j == half - 1, 1.0, 0.0).astype(BF16)
    lane = lax.broadcasted_iota(jnp.int32, (1, table // 2), 1)
    span = 2 * seq
    pieces = []
    for h in range(heads):
        score = nn(flip, gs0[h]) + nn(flip, gs1[h])
        score = jnp.concatenate([score, jnp.zeros_like(score)], axis=1)
        along = over_rows(pltpu.roll(score, span - 2 * (half - 1), 1, stride=2, stride_axis=0))
        lo = jnp.sum(along[:, seq : span - table // 2], axis=1, keepdims=True)
        hi = jnp.sum(along[:, table // 2 : seq], axis=1, keepdims=True)
        pieces.append(along[:, span - table // 2 :] + jnp.where(lane == 0, lo, 0.0))
        pieces.append(along[:, : table // 2] + jnp.where(lane == table // 2 - 1, hi, 0.0))
    small = [t0[r : r + 1, :] + t1[r : r + 1, :] for r in range(4)]
    small += [a0[r : r + 1, :] + a1[r : r + 1, :] for r in range(3)]
    small.append(jnp.concatenate(pieces, axis=1))
    bq = over_rows(gq0[...].astype(F32)) + over_rows(gq1[...].astype(F32))
    bv = over_rows(gv0[...].astype(F32)) + over_rows(gv1[...].astype(F32))
    last = jnp.concatenate([bq, bv, jnp.zeros((1, width - 2 * e), F32)], axis=1)

    def keys(ref):
        ref[:e, :] = tn(gk0[...], tokens[0]) + tn(gk1[...], tokens[1])
        for r, value in enumerate(small):
            ref[e + r : e + r + 1, :] = value

    def outs(ref):
        ref[:e, :] = tn(ctx0[...], ga0[...]) + tn(ctx1[...], ga1[...])
        ref[e:, :] = jnp.broadcast_to(last, (ref.shape[0] - e, width))

    @pl.when(x_bit() == 0)
    def _():
        keys(keep)
        outs(send)

    @pl.when(x_bit() != 0)
    def _():
        outs(keep)
        keys(send)


def token_end(row, count, again, g_first, *refs):
    parts, refs = refs[:count], refs[count + again :]
    result, place, twice, out, done = refs
    total = gathered(parts, place)
    half = g_first.shape[0]
    for s in range(g_first.shape[1] // 128):
        at = slice(s * 128, (s + 1) * 128)
        value = g_first[:, at] * 0.5
        twice[pl.ds(0, half, stride=2), :] = value
        twice[pl.ds(1, half, stride=2), :] = value
        out[:, at] = (total[:, at] + twice[...]).astype(BF16)
    leave = pltpu.make_async_copy(out, result.at[row], done)
    leave.start()
    leave.wait()


def add(a, b, out):
    out[...] = a[...] + b[...]


def add_split(a, b, keep, send):
    own = centre_half()
    keep[...] = a[own] + b[own]
    send[...] = a[1 - own] + b[1 - own]


def choose(mine, got, out):
    @pl.when(in_centre())
    def _():
        out[...] = mine[...]

    @pl.when(jnp.logical_not(in_centre()))
    def _():
        out[...] = got[...]


def ffn_end(kind, lo, count, *refs):
    parts, (outer, inner, *sems) = refs[:count], refs[-4:]

    def lay(which, low, high):
        @pl.when(which)
        def _():
            copies = [
                pltpu.make_async_copy(part, out.at[lo : lo + part.shape[0]], sem)
                for part, out, sem in zip((low, high), (outer, inner), sems, strict=True)
            ]
            for copy in copies:
                copy.start()
            for copy in copies:
                copy.wait()

    if kind == "X":
        lay(x_bit() == 0, parts[0], parts[1])
        lay(x_bit() != 0, parts[1], parts[0])
        return
    for here, one, two in ((in_centre(), *parts[:2]), (jnp.logical_not(in_centre()), *parts[2:])):
        lay(here & (centre_half() == 0), one, two)
        lay(here & (centre_half() == 1), two, one)


def attn_end_one(final, far, wq, wv):
    def lay(query, value):
        wq[...] = query[...]
        wv[...] = value[...]

    @pl.when(x_bit() == 0)
    def _():
        lay(final, far)

    @pl.when(x_bit() != 0)
    def _():
        lay(far, final)


def attn_end_two(final, far, wk, wo, bq, bv, rel, *small):
    e, width = wk.shape
    heads = rel.shape[0]
    table = width // heads

    def lay(one, two):
        wk[...] = one[:e, :]
        wo[...] = two[:e, :]
        for r, ref in enumerate(small):
            ref[...] = one[e + r, :]
        for h in range(heads):
            rel[h : h + 1, :] = one[e + len(small) : e + len(small) + 1, h * table : (h + 1) * table]
        bq[...] = two[e, :e]
        bv[...] = two[e, e : 2 * e]

    @pl.when(x_bit() == 0)
    def _():
        lay(final, far)

    @pl.when(x_bit() != 0)
    def _():
        lay(far, final)


CHUNKS = [("X", 0, 2), ("X", 2, 3), ("X", 3, 4), ("X", 4, 5), ("Z", 5, 6)]


class TensorSum:
    def __init__(self, run, keep, *send):
        self.run, self.keep, self.got = run, keep, [core_swap(a) for a in send]

    def add(self):
        (self.chip,) = self.run(chip_sum, [shape(self.keep.shape)], [self.keep, *self.got])
        self.far = chip_swap(self.chip)

    def tot(self):
        mine = self.run(total_sum, [shape(a.shape) for a in self.got], [self.chip, self.far])
        self.parts = [*mine, *(core_swap(a) for a in mine)]


def others(a, bit):
    while bit < lax.axis_size("dp"):
        a = a + lax.ppermute(a, "dp", swap_pairs(lax.axis_size("dp"), bit))
        bit *= 2
    return a


class XFirst:
    def __init__(self, run, make):
        self.run, self.make_outs = run, make

    def plus(self, pairs):
        (self.mine,) = self.run(add, [shape(self.mine.shape)], [self.mine, self.got])
        self.got = hop(self.mine, pairs) if on_line_of_four() else None

    def make(self):
        self.mine, send = self.make_outs()
        self.got = x_swap(send)

    def xa(self):
        self.plus(INWARD)

    def ia(self):
        if on_line_of_four():
            self.plus(MIDDLE)

    def ma(self):
        if on_line_of_four():
            self.plus(OUTWARD)

    def ch(self):
        if on_line_of_four():
            (self.mine,) = self.run(choose, [shape(self.mine.shape)], [self.mine, self.got])
        else:
            self.mine = others(self.mine, 2)
        self.parts = [self.mine, x_swap(self.mine)]


class ZFirst:
    def __init__(self, run, make):
        self.run, self.make_outs = run, make

    def make(self):
        (self.whole,) = self.make_outs()
        self.got = hop(self.whole, INWARD) if on_line_of_four() else None

    def ia(self):
        if on_line_of_four():
            half = shape(self.whole.shape[1:])
            self.mine, send = self.run(add_split, [half, half], [self.whole, self.got])
            self.got = hop(send, MIDDLE)

    def ma(self):
        if on_line_of_four():
            (self.mine,) = self.run(add, [shape(self.mine.shape)], [self.mine, self.got])
            self.got = hop(self.mine, CENTRE_X)

    def xa(self):
        if on_line_of_four():
            (mine,) = self.run(add, [shape(self.mine.shape)], [self.mine, self.got])
            other = hop(mine, MIDDLE)
            self.parts = [mine, other, hop(mine, OUTWARD), hop(other, OUTWARD)]
        else:
            total, own = others(self.whole, 1), centre_half() == 0
            pair = [jnp.where(own, total[0], total[1]), jnp.where(own, total[1], total[0])]
            self.parts = pair + pair


def local(
    tokens,
    lengths,
    groups,
    key_mask,
    w_query,
    b_query,
    w_key,
    w_value,
    b_value,
    rel_bias,
    w_out,
    b_out,
    gain_one,
    shift_one,
    w_inner,
    b_inner,
    w_outer,
    b_outer,
    gain_two,
    shift_two,
    cotangent,
):
    rows, seq, width = tokens.shape
    half = seq // 2
    heads, table = rel_bias.shape
    e = w_query.shape[1]
    hidden = w_inner.shape[1]
    w_query, w_key, w_value = w_query.T, w_key.T, w_value.T
    run = Line()
    place = lambda n: pltpu.VMEM((n, width), F32)
    dma = pltpu.SemaphoreType.DMA

    def summands(n, piece=PIECE):
        return [shape((n // 2, width))] + [shape((piece, width))] * (n // 2 // piece)

    class Row:
        output = grad_tokens = None

        def __init__(self, r):
            self.r = r

        def attend(self):
            outs = [
                shape((half, e), BF16),
                shape((half, e), BF16),
                shape((seq, e), BF16),
                shape((seq, e), BF16),
                shape((heads, half, seq)),
                shape((half, width)),
            ]
            late = [lengths, (tokens, self.r), groups, key_mask]
            late += [w_query, b_query, w_key, w_value, b_value, rel_bias, w_out]
            got = run(functools.partial(attend, self.r), outs + summands(half), [], late=late)
            self.ctx, self.q, self.k, self.v, self.prob, self.pooled = got[:6]
            self.att = TensorSum(run, *got[6:])

        def forward(self):
            outs = [
                shape((half, width)),
                shape((half, 1)),
                shape((half, width), BF16),
                shape((half, hidden), BF16),
                shape((half, hidden)),
            ]
            parts = self.att.parts
            got = run(
                functools.partial(forward, len(parts)),
                outs + summands(half),
                [self.pooled, *parts],
                late=[b_out, gain_one, shift_one, w_inner, b_inner, w_outer],
                scratch=[place(half)],
            )
            self.normed, self.factor, self.y_low, self.act, self.slope = got[:5]
            self.ffn = TensorSum(run, *got[5:])

        def turn(self):
            outs = [
                shape((rows, half, width), BF16),
                shape((half, width)),
                shape((half, width), BF16),
                shape((half, hidden), BF16),
                shape((8, width)),
            ]
            parts = self.ffn.parts
            before = [] if Row.output is None else [Row.output]
            got = run(
                functools.partial(turn, self.r, len(parts), len(before)),
                outs + summands(half),
                [self.normed, self.slope, *parts, *before],
                late=[gain_one, shift_one, b_outer, gain_two, shift_two, (cotangent, self.r), w_outer, w_inner],
                scratch=[place(half), pltpu.VMEM((half, width), BF16), dma],
                left=(0,),
                onto=[2 + len(parts)] if before else (),
            )
            Row.output, self.g_second, self.g_ffn, self.g_inner, self.t_small = got[:5]
            self.back = TensorSum(run, *got[5:])

        def aback(self):
            outs = [
                shape((half, width)),
                shape((half, width), BF16),
                shape((heads, half, seq), BF16),
                shape((half, e), BF16),
                shape((seq, e), BF16),
                shape((seq, e), BF16),
                shape((8, width)),
            ]
            parts = self.back.parts
            got = run(
                functools.partial(attend_back, heads, len(parts)),
                outs + summands(seq, seq // 2),
                [self.g_second, self.normed, self.factor, self.q, self.k, self.v, self.prob, *parts],
                late=[gain_one, w_out, w_query, w_key, w_value],
                scratch=[place(half)],
            )
            self.g_first, self.g_attn, self.gs, self.gq, self.gk, self.gv, self.a_small = got[:7]
            self.tok = TensorSum(run, *got[7:])

        def tokend(self):
            parts = self.tok.parts
            before = [] if Row.grad_tokens is None else [Row.grad_tokens]
            (Row.grad_tokens,) = run(
                functools.partial(token_end, self.r, len(parts), len(before)),
                [shape((rows, seq, width), BF16)],
                [self.g_first, *parts, *before],
                scratch=[place(seq), pltpu.VMEM((seq, 128), F32), pltpu.VMEM((seq, width), BF16), dma],
                left=(0,),
                onto=[1 + len(parts)] if before else (),
            )

    r0, r1 = (Row(r) for r in range(rows))

    def ffn_chunk(kind, lo, hi):
        def make():
            outs = [shape((hi - lo, width))] * 2 if kind == "X" else [shape((2, hi - lo, width))]
            ins = [r0.act, r1.act, r0.g_ffn, r1.g_ffn, r0.y_low, r1.y_low, r0.g_inner, r1.g_inner]
            return run(functools.partial(ffn_weights, kind, lo, hi), outs, ins)

        return (XFirst if kind == "X" else ZFirst)(run, make)

    cuts = [(kind, lo * width // 6, hi * width // 6) for kind, lo, hi in CHUNKS]
    chunks = [ffn_chunk(*cut) for cut in cuts]
    x, z = ([chunk for chunk in chunks if isinstance(chunk, kind)] for kind in (XFirst, ZFirst))

    def attn_one():
        ins = [tokens, r0.gq, r1.gq, r0.gv, r1.gv, r0.pooled, r1.pooled]
        return run(attn_weights_one, [shape((e, width))] * 2, ins)

    def attn_two():
        ins = [tokens, r0.gq, r1.gq, r0.gk, r1.gk, r0.gv, r1.gv, r0.ctx, r1.ctx, r0.g_attn, r1.g_attn]
        ins += [r0.gs, r1.gs, r0.t_small, r1.t_small, r0.a_small, r1.a_small]
        return run(functools.partial(attn_weights_two, heads, table), [shape((e + 8, width))] * 2, ins)

    a = [XFirst(run, attn_one), XFirst(run, attn_two)]

    class Ffn:
        grads = ()

    def end(chunk):
        cut = cuts[chunks.index(chunk)]
        outs = [shape((hidden, width)), shape((width, hidden))]
        count = len(chunk.parts)
        Ffn.grads = run(
            functools.partial(ffn_end, *cut[:2], count),
            outs,
            [*chunk.parts, *Ffn.grads],
            scratch=[dma, dma],
            left=(0, 1),
            onto=[count, count + 1] if Ffn.grads else (),
        )

    def aend0():
        return run(attn_end_one, [shape((e, width))] * 2, a[0].parts)

    def aend1():
        outs = [shape((e, width))] * 2 + [shape((e,)), shape((e,)), shape((heads, table))] + [shape((width,))] * 7
        return run(attn_end_two, outs, a[1].parts)

    r0.attend()
    r0.att.add()
    r1.attend()
    r1.att.add()
    r0.att.tot()
    r0.forward()
    r0.ffn.add()
    r1.att.tot()
    r1.forward()
    r1.ffn.add()
    r0.ffn.tot()
    r0.turn()
    r0.back.add()
    r1.ffn.tot()
    r1.turn()
    x[1].make()
    z[0].make()
    x[2].make()
    r1.back.add()
    r0.back.tot()
    x[0].make()
    x[1].xa()
    r0.aback()
    x[2].xa()
    r1.back.tot()
    z[0].ia()
    r1.aback()
    a[0].make()
    x[2].ia()
    z[0].ma()
    r0.tok.add()
    x[0].xa()
    x[1].ia()
    x[2].ma()
    a[1].make()
    x[1].ma()
    a[0].xa()
    x[2].ch()
    x[0].ia()
    x[3].make()
    r0.tok.tot()
    a[1].xa()
    a[0].ia()
    x[3].xa()
    r1.tok.add()
    x[0].ma()
    x[1].ch()
    a[1].ia()
    z[0].xa()
    a[0].ma()
    end(x[2])
    x[0].ch()
    r0.tokend()
    end(x[1])
    a[1].ma()
    a[0].ch()
    x[3].ia()
    end(x[0])
    a[1].ch()
    r1.tok.tot()
    x[3].ma()
    x[3].ch()
    grad_w_query, grad_w_value = aend0()
    grad_w_key, grad_w_out, grad_b_query, grad_b_value, grad_rel_bias, *small = aend1()
    r1.tokend()
    end(z[0])
    end(x[3])
    grad_w_outer, grad_w_inner = Ffn.grads
    grad_b_inner, grad_b_outer, grad_gain_two, grad_shift_two, grad_gain_one, grad_shift_one, grad_b_out = small
    return (
        Row.output,
        Row.grad_tokens,
        grad_w_query.T,
        grad_b_query,
        grad_w_key.T,
        grad_w_value.T,
        grad_b_value,
        grad_rel_bias,
        grad_w_out,
        grad_b_out,
        grad_gain_one,
        grad_shift_one,
        grad_w_inner,
        grad_b_inner,
        grad_w_outer,
        grad_b_outer,
        grad_gain_two,
        grad_shift_two,
    )


def solution(mesh):
    placed = (
        P("dp", None, None),
        P("dp"),
        P("dp", None),
        P("dp", None),
        P(None, "tensor"),
        P("tensor"),
        P(None, "tensor"),
        P(None, "tensor"),
        P("tensor"),
        P("tensor", None),
        P("tensor", None),
        P(),
        P(),
        P(),
        P(None, "tensor"),
        P("tensor"),
        P("tensor", None),
        P(),
        P(),
        P(),
        P("dp", None, None),
    )
    return jax.shard_map(
        local,
        mesh=mesh,
        in_specs=placed,
        out_specs=(
            P("dp", None, None),
            P("dp", None, None),
            P(None, "tensor"),
            P("tensor"),
            P(None, "tensor"),
            P(None, "tensor"),
            P("tensor"),
            P("tensor", None),
            P("tensor", None),
            P(),
            P(),
            P(),
            P(None, "tensor"),
            P("tensor"),
            P("tensor", None),
            P(),
            P(),
            P(),
        ),
        check_vma=False,
    )
```

profile of v0, /device:TPU:0, one launch (start us, length us, event | category | flops | bytes accessed | tf_op | source)
XLA Modules:
  0.0 213.9 jit_solution(15293307292828821782)
XLA Ops:
  3.1 2.3 %attend.2 = (bf16[256,192]{1,0:T(8,128)(2,1)S(1)}, bf16[256,192]{1,0:T(8,128)(2,1)S(1)}, bf16[512,192]{1,0:T(8,128)(2,1)S(1)}, bf16[512,192]{1,0:T(8,128)(2,1)S(...) custom-call(s32[2]{0:T(128)S(1)} %copy-done.21, ...), custom_call_target="tpu_custom_call" | custom-call | flops 1024 | bytes 1024 | tf_op jit(solution)/shard_map/attend/pallas_call | solution.py:114
  8.0 2.7 %collective-permute-start.9 = (f32[128,768]{1,0:T(8,128)S(1)}, f32[128,768]{1,0:T(8,128)S(1)}, u32[]{:S(2)}, u32[]{:S(2)}) collective-permute-start(f32[128,768]{1,0:T(8,128)S(1)} %get-tuple-element.281.refs_0_), channel_id=1, source_target_pairs={{0,2},{1,3},{2,0},{3,1},{4,6},{5,7},{6,4},{7,5},{8,10},{9,11},{10,... | collective-permute-start | bytes 1179656 | tf_op jit(solution)/shard_map/ppermute | solution.py:30
  10.7 2.3 %attend.3 = (bf16[256,192]{1,0:T(8,128)(2,1)S(1)}, bf16[256,192]{1,0:T(8,128)(2,1)S(1)}, bf16[512,192]{1,0:T(8,128)(2,1)S(1)}, bf16[512,192]{1,0:T(8,128)(2,1)S(...) custom-call(s32[2]{0:T(128)S(1)} %copy-done.21, ...), custom_call_target="tpu_custom_call" | custom-call | flops 1024 | bytes 1024 | tf_op jit(solution)/shard_map/attend/pallas_call | solution.py:114
  15.4 5.2 %collective-permute-done.9.refs_1_ = f32[128,768]{1,0:T(8,128)S(1)} collective-permute-done((f32[128,768]{1,0:T(8,128)S(1)}, f32[128,768]{1,0:T(8,128)S(1)}, u32[]{:S(2)}, u32[]{:S(2)}) %collective-permute-start.9) | collective-permute-done | bytes 393248 | tf_op jit(solution)/shard_map/ppermute | solution.py:30
  26.5 2.0 collective-permute-start.27
  34.6 1.8 collective-permute-start.26
  36.4 2.1 collective-permute-done.27.refs_1_
  40.6 2.0 turn.2
  47.6 1.7 collective-permute-start.46
  49.3 2.0 turn.3
  53.7 3.5 %collective-permute-start.56 = (f32[2,128,768]{2,1,0:T(8,128)S(1)}, f32[2,128,768]{2,1,0:T(8,128)S(1)}, u32[]{:S(2)}, u32[]{:S(2)}) collective-permute-start(f32[2,128,768]{2,1,0:T(8,128)S(1)} %get-tuple-element.381.refs_0_), channel_id=1, source_target_pairs={{0,8},{4,12},{24,16},{28,20},{1,9},{5,13},{25,17},{29,21},{2,10},{... | collective-permute-start | bytes 2359304 | tf_op jit(solution)/shard_map/ppermute | solution.py:38
  65.3 3.3 %attend_back.2 = (f32[256,768]{1,0:T(8,128)S(1)}, bf16[256,768]{1,0:T(8,128)(2,1)S(1)}, bf16[3,256,512]{2,1,0:T(8,128)(2,1)S(1)}, bf16[256,192]{1,0:T(8,128)(2,1...) custom-call(f32[768]{0:T(1024)S(1)} %copy-done.8, ...), custom_call_target="tpu_custom_call" | custom-call | flops 1024 | bytes 1024 | tf_op jit(solution)/shard_map/attend_back/pallas_call | solution.py:114
  68.8 2.4 %collective-permute-start.58 = (f32[256,768]{1,0:T(8,128)S(1)}, f32[256,768]{1,0:T(8,128)S(1)}, u32[]{:S(2)}, u32[]{:S(2)}) collective-permute-start(f32[256,768]{1,0:T(8,128)S(1)} %get-tuple-element.388), channel_id=1, source_target_pairs={{0,4},{4,0},{8,12},{12,8},{16,20},{20,16},{24,28},{28,24},{1,5},{5... | collective-permute-start | bytes 2359304 | tf_op jit(solution)/shard_map/ppermute | solution.py:34
  71.7 3.5 %collective-permute-start.61 = (f32[128,768]{1,0:T(8,128)S(1)}, f32[128,768]{1,0:T(8,128)S(1)}, u32[]{:S(2)}, u32[]{:S(2)}) collective-permute-start(f32[128,768]{1,0:T(8,128)S(1)} %get-tuple-element.393.refs_0_), channel_id=1, source_target_pairs={{0,8},{4,12},{24,16},{28,20},{1,9},{5,13},{25,17},{29,21},{2,10},{... | collective-permute-start | bytes 1179656 | tf_op jit(solution)/shard_map/ppermute | solution.py:38
  78.7 4.6 %collective-permute-start.64 = (f32[128,768]{1,0:T(8,128)S(1)}, f32[128,768]{1,0:T(8,128)S(1)}, u32[]{:S(2)}, u32[]{:S(2)}) collective-permute-start(f32[128,768]{1,0:T(8,128)S(1)} %get-tuple-element.405.refs_0_), channel_id=1, source_target_pairs={{0,8},{4,12},{24,16},{28,20},{1,9},{5,13},{25,17},{29,21},{2,10},{... | collective-permute-start | bytes 1179656 | tf_op jit(solution)/shard_map/ppermute | solution.py:38
  83.3 3.3 %attend_back.3 = (f32[256,768]{1,0:T(8,128)S(1)}, bf16[256,768]{1,0:T(8,128)(2,1)S(1)}, bf16[3,256,512]{2,1,0:T(8,128)(2,1)S(1)}, bf16[256,192]{1,0:T(8,128)(2,1...) custom-call(f32[768]{0:T(1024)S(1)} %copy-done.8, ...), custom_call_target="tpu_custom_call" | custom-call | flops 1024 | bytes 1024 | tf_op jit(solution)/shard_map/attend_back/pallas_call | solution.py:114
  89.3 4.1 %collective-permute-start.62 = (f32[256,768]{1,0:T(8,128)S(1)}, f32[256,768]{1,0:T(8,128)S(1)}, u32[]{:S(2)}, u32[]{:S(2)}) collective-permute-start(f32[256,768]{1,0:T(8,128)S(1)} %get-tuple-element.403.refs_0_), channel_id=1, source_target_pairs={{0,8},{4,12},{24,16},{28,20},{1,9},{5,13},{25,17},{29,21},{2,10},{... | collective-permute-start | bytes 2359304 | tf_op jit(solution)/shard_map/ppermute | solution.py:38
  98.0 1.7 attn_weights_two.1
  100.3 9.4 %collective-permute-done.66.refs_1_ = f32[192,768]{1,0:T(8,128)S(1)} collective-permute-done((f32[192,768]{1,0:T(8,128)S(1)}, f32[192,768]{1,0:T(8,128)S(1)}, u32[]{:S(2)}, u32[]{:S(2)}) %collective-permute-start.66) | collective-permute-done | bytes 589856 | tf_op jit(solution)/shard_map/ppermute | solution.py:34
  112.7 2.9 %collective-permute-done.71.refs_1_ = f32[256,768]{1,0:T(8,128)S(1)} collective-permute-done((f32[256,768]{1,0:T(8,128)S(1)}, f32[256,768]{1,0:T(8,128)S(1)}, u32[]{:S(2)}, u32[]{:S(2)}) %collective-permute-start.71) | collective-permute-done | bytes 786464 | tf_op jit(solution)/shard_map/ppermute | solution.py:30
  116.2 6.7 %collective-permute-done.70.refs_1_ = f32[200,768]{1,0:T(8,128)S(1)} collective-permute-done((f32[200,768]{1,0:T(8,128)S(1)}, f32[200,768]{1,0:T(8,128)S(1)}, u32[]{:S(2)}, u32[]{:S(2)}) %collective-permute-start.70) | collective-permute-done | bytes 614432 | tf_op jit(solution)/shard_map/ppermute | solution.py:34
  123.0 4.2 %collective-permute-start.73 = (f32[200,768]{1,0:T(8,128)S(1)}, f32[200,768]{1,0:T(8,128)S(1)}, u32[]{:S(2)}, u32[]{:S(2)}) collective-permute-start(f32[200,768]{1,0:T(8,128)S(1)} %get-tuple-element.442.refs_0_), channel_id=1, source_target_pairs={{0,8},{4,12},{24,16},{28,20},{1,9},{5,13},{25,17},{29,21},{2,10},{... | collective-permute-start | bytes 1843208 | tf_op jit(solution)/shard_map/ppermute | solution.py:38
  131.8 7.1 %collective-permute-done.74.refs_1_ = f32[128,768]{1,0:T(8,128)S(1)} collective-permute-done((f32[128,768]{1,0:T(8,128)S(1)}, f32[128,768]{1,0:T(8,128)S(1)}, u32[]{:S(2)}, u32[]{:S(2)}) %collective-permute-start.74) | collective-permute-done | bytes 393248 | tf_op jit(solution)/shard_map/ppermute | solution.py:38
  139.8 2.1 collective-permute-start.77
  142.0 8.9 %collective-permute-done.78.refs_1_ = f32[128,768]{1,0:T(8,128)S(1)} collective-permute-done((f32[128,768]{1,0:T(8,128)S(1)}, f32[128,768]{1,0:T(8,128)S(1)}, u32[]{:S(2)}, u32[]{:S(2)}) %collective-permute-start.78) | collective-permute-done | bytes 393248 | tf_op jit(solution)/shard_map/ppermute | solution.py:34
  156.1 3.1 %collective-permute-done.77.refs_1_ = f32[128,768]{1,0:T(8,128)S(1)} collective-permute-done((f32[128,768]{1,0:T(8,128)S(1)}, f32[128,768]{1,0:T(8,128)S(1)}, u32[]{:S(2)}, u32[]{:S(2)}) %collective-permute-start.77) | collective-permute-done | bytes 393248 | tf_op jit(solution)/shard_map/ppermute | solution.py:34
  159.3 5.1 %collective-permute-start.85 = (f32[128,768]{1,0:T(8,128)S(1)}, f32[128,768]{1,0:T(8,128)S(1)}, u32[]{:S(2)}, u32[]{:S(2)}) collective-permute-start(f32[128,768]{1,0:T(8,128)S(1)} %get-tuple-element.469.refs_0_), channel_id=1, source_target_pairs={{0,8},{4,12},{24,16},{28,20},{1,9},{5,13},{25,17},{29,21},{2,10},{... | collective-permute-start | bytes 1179656 | tf_op jit(solution)/shard_map/ppermute | solution.py:38
  171.7 4.4 %collective-permute-done.84.refs_1_ = f32[256,768]{1,0:T(8,128)S(1)} collective-permute-done((f32[256,768]{1,0:T(8,128)S(1)}, f32[256,768]{1,0:T(8,128)S(1)}, u32[]{:S(2)}, u32[]{:S(2)}) %collective-permute-start.84) | collective-permute-done | bytes 786464 | tf_op jit(solution)/shard_map/ppermute | solution.py:34
  178.0 2.6 %collective-permute-done.83.refs_1_ = f32[200,768]{1,0:T(8,128)S(1)} collective-permute-done((f32[200,768]{1,0:T(8,128)S(1)}, f32[200,768]{1,0:T(8,128)S(1)}, u32[]{:S(2)}, u32[]{:S(2)}) %collective-permute-start.83) | collective-permute-done | bytes 614432 | tf_op jit(solution)/shard_map/ppermute | solution.py:38
  184.5 10.8 %collective-permute-done.91.refs_1_ = f32[128,768]{1,0:T(8,128)S(1)} collective-permute-done((f32[128,768]{1,0:T(8,128)S(1)}, f32[128,768]{1,0:T(8,128)S(1)}, u32[]{:S(2)}, u32[]{:S(2)}) %collective-permute-start.91) | collective-permute-done | bytes 393248 | tf_op jit(solution)/shard_map/ppermute | solution.py:38
  198.5 3.4 %collective-permute-done.88.refs_1_ = f32[200,768]{1,0:T(8,128)S(1)} collective-permute-done((f32[200,768]{1,0:T(8,128)S(1)}, f32[200,768]{1,0:T(8,128)S(1)}, u32[]{:S(2)}, u32[]{:S(2)}) %collective-permute-start.88) | collective-permute-done | bytes 614432 | tf_op jit(solution)/shard_map/ppermute | solution.py:34
  204.4 7.5 %collective-permute-done.95.refs_3_ = f32[128,768]{1,0:T(8,128)S(1)} collective-permute-done((f32[128,768]{1,0:T(8,128)S(1)}, f32[128,768]{1,0:T(8,128)S(1)}, u32[]{:S(2)}, u32[]{:S(2)}) %collective-permute-start.95) | collective-permute-done | bytes 393248 | tf_op jit(solution)/shard_map/ppermute | solution.py:38
  (272 shorter events, 82.9 us)
Async XLA Ops:
  15.1 13.6 %collective-permute-start.8 = (f32[128,768]{1,0:T(8,128)S(1)}, f32[128,768]{1,0:T(8,128)S(1)}, u32[]{:S(2)}, u32[]{:S(2)}) collective-permute-start(f32[128,768]{1,0:T(8,128)S(1)} %get-tuple-element.279.refs_0_), channel_id=1, source_target_pairs={{0,2},{1,3},{2,0},{3,1},{4,6},{5,7},{6,4},{7,5},{8,10},{9,11},{10,... | collective-permute-start | bytes 1179656 | tf_op jit(solution)/shard_map/ppermute | solution.py:30
  47.6 13.9 %collective-permute-start.46 = (f32[128,768]{1,0:T(8,128)S(1)}, f32[128,768]{1,0:T(8,128)S(1)}, u32[]{:S(2)}, u32[]{:S(2)}) collective-permute-start(f32[128,768]{1,0:T(8,128)S(1)} %get-tuple-element.364.refs_0_), channel_id=1, source_target_pairs={{0,2},{1,3},{2,0},{3,1},{4,6},{5,7},{6,4},{7,5},{8,10},{9,11},{10,... | collective-permute-start | bytes 1179656 | tf_op jit(solution)/shard_map/ppermute | solution.py:30
  53.7 21.8 %collective-permute-start.56 = (f32[2,128,768]{2,1,0:T(8,128)S(1)}, f32[2,128,768]{2,1,0:T(8,128)S(1)}, u32[]{:S(2)}, u32[]{:S(2)}) collective-permute-start(f32[2,128,768]{2,1,0:T(8,128)S(1)} %get-tuple-element.381.refs_0_), channel_id=1, source_target_pairs={{0,8},{4,12},{24,16},{28,20},{1,9},{5,13},{25,17},{29,21},{2,10},{... | collective-permute-start | bytes 2359304 | tf_op jit(solution)/shard_map/ppermute | solution.py:38
  68.6 19.6 %collective-permute-start.59 = (f32[256,768]{1,0:T(8,128)S(1)}, f32[256,768]{1,0:T(8,128)S(1)}, u32[]{:S(2)}, u32[]{:S(2)}) collective-permute-start(f32[256,768]{1,0:T(8,128)S(1)} %get-tuple-element.390), channel_id=1, source_target_pairs={{0,1},{1,0},{2,3},{3,2},{4,5},{5,4},{6,7},{7,6},{8,9},{9,8},{10,11... | collective-permute-start | bytes 2359304 | tf_op jit(solution)/shard_map/ppermute | solution.py:26
  68.8 20.4 %collective-permute-start.58 = (f32[256,768]{1,0:T(8,128)S(1)}, f32[256,768]{1,0:T(8,128)S(1)}, u32[]{:S(2)}, u32[]{:S(2)}) collective-permute-start(f32[256,768]{1,0:T(8,128)S(1)} %get-tuple-element.388), channel_id=1, source_target_pairs={{0,4},{4,0},{8,12},{12,8},{16,20},{20,16},{24,28},{28,24},{1,5},{5... | collective-permute-start | bytes 2359304 | tf_op jit(solution)/shard_map/ppermute | solution.py:34
  71.7 15.6 %collective-permute-start.61 = (f32[128,768]{1,0:T(8,128)S(1)}, f32[128,768]{1,0:T(8,128)S(1)}, u32[]{:S(2)}, u32[]{:S(2)}) collective-permute-start(f32[128,768]{1,0:T(8,128)S(1)} %get-tuple-element.393.refs_0_), channel_id=1, source_target_pairs={{0,8},{4,12},{24,16},{28,20},{1,9},{5,13},{25,17},{29,21},{2,10},{... | collective-permute-start | bytes 1179656 | tf_op jit(solution)/shard_map/ppermute | solution.py:38
  78.7 16.3 %collective-permute-start.64 = (f32[128,768]{1,0:T(8,128)S(1)}, f32[128,768]{1,0:T(8,128)S(1)}, u32[]{:S(2)}, u32[]{:S(2)}) collective-permute-start(f32[128,768]{1,0:T(8,128)S(1)} %get-tuple-element.405.refs_0_), channel_id=1, source_target_pairs={{0,8},{4,12},{24,16},{28,20},{1,9},{5,13},{25,17},{29,21},{2,10},{... | collective-permute-start | bytes 1179656 | tf_op jit(solution)/shard_map/ppermute | solution.py:38
  89.3 22.1 %collective-permute-start.62 = (f32[256,768]{1,0:T(8,128)S(1)}, f32[256,768]{1,0:T(8,128)S(1)}, u32[]{:S(2)}, u32[]{:S(2)}) collective-permute-start(f32[256,768]{1,0:T(8,128)S(1)} %get-tuple-element.403.refs_0_), channel_id=1, source_target_pairs={{0,8},{4,12},{24,16},{28,20},{1,9},{5,13},{25,17},{29,21},{2,10},{... | collective-permute-start | bytes 2359304 | tf_op jit(solution)/shard_map/ppermute | solution.py:38
  93.4 16.3 %collective-permute-start.66 = (f32[192,768]{1,0:T(8,128)S(1)}, f32[192,768]{1,0:T(8,128)S(1)}, u32[]{:S(2)}, u32[]{:S(2)}) collective-permute-start(f32[192,768]{1,0:T(8,128)S(1)} %get-tuple-element.410), channel_id=1, source_target_pairs={{0,4},{4,0},{8,12},{12,8},{16,20},{20,16},{24,28},{28,24},{1,5},{5... | collective-permute-start | bytes 1769480 | tf_op jit(solution)/shard_map/ppermute | solution.py:34
  95.8 15.5 %collective-permute-start.65 = (f32[128,768]{1,0:T(8,128)S(1)}, f32[128,768]{1,0:T(8,128)S(1)}, u32[]{:S(2)}, u32[]{:S(2)}) collective-permute-start(f32[128,768]{1,0:T(8,128)S(1)} %get-tuple-element.408.refs_0_), channel_id=1, source_target_pairs={{8,0},{12,4},{16,24},{20,28},{9,1},{13,5},{17,25},{21,29},{10,2},{... | collective-permute-start | bytes 1179656 | tf_op jit(solution)/shard_map/ppermute | solution.py:38
  97.1 18.5 %collective-permute-start.71 = (f32[256,768]{1,0:T(8,128)S(1)}, f32[256,768]{1,0:T(8,128)S(1)}, u32[]{:S(2)}, u32[]{:S(2)}) collective-permute-start(f32[256,768]{1,0:T(8,128)S(1)} %get-tuple-element.435.refs_0_), channel_id=1, source_target_pairs={{0,2},{1,3},{2,0},{3,1},{4,6},{5,7},{6,4},{7,5},{8,10},{9,11},{10,... | collective-permute-start | bytes 2359304 | tf_op jit(solution)/shard_map/ppermute | solution.py:30
  99.7 23.3 %collective-permute-start.70 = (f32[200,768]{1,0:T(8,128)S(1)}, f32[200,768]{1,0:T(8,128)S(1)}, u32[]{:S(2)}, u32[]{:S(2)}) collective-permute-start(f32[200,768]{1,0:T(8,128)S(1)} %get-tuple-element.434), channel_id=1, source_target_pairs={{0,4},{4,0},{8,12},{12,8},{16,20},{20,16},{24,28},{28,24},{1,5},{5... | collective-permute-start | bytes 1843208 | tf_op jit(solution)/shard_map/ppermute | solution.py:34
  109.8 17.4 %collective-permute-start.69 = (f32[192,768]{1,0:T(8,128)S(1)}, f32[192,768]{1,0:T(8,128)S(1)}, u32[]{:S(2)}, u32[]{:S(2)}) collective-permute-start(f32[192,768]{1,0:T(8,128)S(1)} %get-tuple-element.432.refs_0_), channel_id=1, source_target_pairs={{0,8},{4,12},{24,16},{28,20},{1,9},{5,13},{25,17},{29,21},{2,10},{... | collective-permute-start | bytes 1769480 | tf_op jit(solution)/shard_map/ppermute | solution.py:38
  111.3 17.3 %collective-permute-start.57 = (f32[256,768]{1,0:T(8,128)S(1)}, f32[256,768]{1,0:T(8,128)S(1)}, u32[]{:S(2)}, u32[]{:S(2)}) collective-permute-start(f32[256,768]{1,0:T(8,128)S(1)} %get-tuple-element.386), channel_id=1, source_target_pairs={{0,1},{1,0},{2,3},{3,2},{4,5},{5,4},{6,7},{7,6},{8,9},{9,8},{10,11... | collective-permute-start | bytes 2359304 | tf_op jit(solution)/shard_map/ppermute | solution.py:26
  111.5 18.9 %collective-permute-start.75 = (f32[256,768]{1,0:T(8,128)S(1)}, f32[256,768]{1,0:T(8,128)S(1)}, u32[]{:S(2)}, u32[]{:S(2)}) collective-permute-start(f32[256,768]{1,0:T(8,128)S(1)} %get-tuple-element.444.refs_0_), channel_id=1, source_target_pairs={{8,16},{12,20},{16,8},{20,12},{9,17},{13,21},{17,9},{21,13},{10,18... | collective-permute-start | bytes 2359304 | tf_op jit(solution)/shard_map/ppermute | solution.py:38
  115.6 14.0 %collective-permute-start.68 = (f32[128,768]{1,0:T(8,128)S(1)}, f32[128,768]{1,0:T(8,128)S(1)}, u32[]{:S(2)}, u32[]{:S(2)}) collective-permute-start(f32[128,768]{1,0:T(8,128)S(1)} %get-tuple-element.431), channel_id=1, source_target_pairs={{0,4},{4,0},{8,12},{12,8},{16,20},{20,16},{24,28},{28,24},{1,5},{5... | collective-permute-start | bytes 1179656 | tf_op jit(solution)/shard_map/ppermute | solution.py:34
  123.0 15.9 %collective-permute-start.73 = (f32[200,768]{1,0:T(8,128)S(1)}, f32[200,768]{1,0:T(8,128)S(1)}, u32[]{:S(2)}, u32[]{:S(2)}) collective-permute-start(f32[200,768]{1,0:T(8,128)S(1)} %get-tuple-element.442.refs_0_), channel_id=1, source_target_pairs={{0,8},{4,12},{24,16},{28,20},{1,9},{5,13},{25,17},{29,21},{2,10},{... | collective-permute-start | bytes 1843208 | tf_op jit(solution)/shard_map/ppermute | solution.py:38
  130.5 23.2 %collective-permute-start.82 = (f32[256,768]{1,0:T(8,128)S(1)}, f32[256,768]{1,0:T(8,128)S(1)}, u32[]{:S(2)}, u32[]{:S(2)}) collective-permute-start(f32[256,768]{1,0:T(8,128)S(1)} %get-tuple-element.460.refs_0_), channel_id=1, source_target_pairs={{8,0},{12,4},{16,24},{20,28},{9,1},{13,5},{17,25},{21,29},{10,2},{... | collective-permute-start | bytes 2359304 | tf_op jit(solution)/shard_map/ppermute | solution.py:38
  138.9 15.8 %collective-permute-start.81 = (f32[256,768]{1,0:T(8,128)S(1)}, f32[256,768]{1,0:T(8,128)S(1)}, u32[]{:S(2)}, u32[]{:S(2)}) collective-permute-start(f32[256,768]{1,0:T(8,128)S(1)} %get-tuple-element.459.refs_1_), channel_id=1, source_target_pairs={{0,1},{1,0},{2,3},{3,2},{4,5},{5,4},{6,7},{7,6},{8,9},{9,8},{10,11... | collective-permute-start | bytes 2359304 | tf_op jit(solution)/shard_map/ppermute | solution.py:26
  139.1 27.5 %collective-permute-start.76 = (f32[200,768]{1,0:T(8,128)S(1)}, f32[200,768]{1,0:T(8,128)S(1)}, u32[]{:S(2)}, u32[]{:S(2)}) collective-permute-start(f32[200,768]{1,0:T(8,128)S(1)} %get-tuple-element.448.refs_0_), channel_id=1, source_target_pairs={{8,16},{12,20},{16,8},{20,12},{9,17},{13,21},{17,9},{21,13},{10,18... | collective-permute-start | bytes 1843208 | tf_op jit(solution)/shard_map/ppermute | solution.py:38
  139.8 19.5 %collective-permute-start.77 = (f32[128,768]{1,0:T(8,128)S(1)}, f32[128,768]{1,0:T(8,128)S(1)}, u32[]{:S(2)}, u32[]{:S(2)}) collective-permute-start(f32[128,768]{1,0:T(8,128)S(1)} %get-tuple-element.449.refs_0_), channel_id=1, source_target_pairs={{0,4},{4,0},{8,12},{12,8},{16,20},{20,16},{24,28},{28,24},{1,5},{5... | collective-permute-start | bytes 1179656 | tf_op jit(solution)/shard_map/ppermute | solution.py:34
  150.8 17.2 %collective-permute-start.86 = (f32[192,768]{1,0:T(8,128)S(1)}, f32[192,768]{1,0:T(8,128)S(1)}, u32[]{:S(2)}, u32[]{:S(2)}) collective-permute-start(f32[192,768]{1,0:T(8,128)S(1)} %get-tuple-element.470.refs_0_), channel_id=1, source_target_pairs={{8,0},{12,4},{16,24},{20,28},{9,1},{13,5},{17,25},{21,29},{10,2},{... | collective-permute-start | bytes 1769480 | tf_op jit(solution)/shard_map/ppermute | solution.py:38
  153.8 22.3 %collective-permute-start.84 = (f32[256,768]{1,0:T(8,128)S(1)}, f32[256,768]{1,0:T(8,128)S(1)}, u32[]{:S(2)}, u32[]{:S(2)}) collective-permute-start(f32[256,768]{1,0:T(8,128)S(1)} %get-tuple-element.466.refs_0_), channel_id=1, source_target_pairs={{0,4},{4,0},{8,12},{12,8},{16,20},{20,16},{24,28},{28,24},{1,5},{5... | collective-permute-start | bytes 2359304 | tf_op jit(solution)/shard_map/ppermute | solution.py:34
  154.7 25.9 %collective-permute-start.72 = (f32[256,768]{1,0:T(8,128)S(1)}, f32[256,768]{1,0:T(8,128)S(1)}, u32[]{:S(2)}, u32[]{:S(2)}) collective-permute-start(f32[256,768]{1,0:T(8,128)S(1)} %get-tuple-element.441.refs_0_), channel_id=1, source_target_pairs={{0,2},{1,3},{2,0},{3,1},{4,6},{5,7},{6,4},{7,5},{8,10},{9,11},{10,... | collective-permute-start | bytes 2359304 | tf_op jit(solution)/shard_map/ppermute | solution.py:30
  166.7 13.9 %collective-permute-start.83 = (f32[200,768]{1,0:T(8,128)S(1)}, f32[200,768]{1,0:T(8,128)S(1)}, u32[]{:S(2)}, u32[]{:S(2)}) collective-permute-start(f32[200,768]{1,0:T(8,128)S(1)} %get-tuple-element.465.refs_0_), channel_id=1, source_target_pairs={{8,0},{12,4},{16,24},{20,28},{9,1},{13,5},{17,25},{21,29},{10,2},{... | collective-permute-start | bytes 1843208 | tf_op jit(solution)/shard_map/ppermute | solution.py:38
  170.4 26.2 %collective-permute-start.89 = (f32[192,768]{1,0:T(8,128)S(1)}, f32[192,768]{1,0:T(8,128)S(1)}, u32[]{:S(2)}, u32[]{:S(2)}) collective-permute-start(f32[192,768]{1,0:T(8,128)S(1)} %get-tuple-element.479.refs_0_), channel_id=1, source_target_pairs={{0,4},{4,0},{8,12},{12,8},{16,20},{20,16},{24,28},{28,24},{1,5},{5... | collective-permute-start | bytes 1769480 | tf_op jit(solution)/shard_map/ppermute | solution.py:34
  180.7 22.4 %collective-permute-start.87 = (f32[256,768]{1,0:T(8,128)S(1)}, f32[256,768]{1,0:T(8,128)S(1)}, u32[]{:S(2)}, u32[]{:S(2)}) collective-permute-start(f32[256,768]{1,0:T(8,128)S(1)} %get-tuple-element.476.refs_1_), channel_id=1, source_target_pairs={{0,1},{1,0},{2,3},{3,2},{4,5},{5,4},{6,7},{7,6},{8,9},{9,8},{10,11... | collective-permute-start | bytes 2359304 | tf_op jit(solution)/shard_map/ppermute | solution.py:26
  180.9 14.4 %collective-permute-start.91 = (f32[128,768]{1,0:T(8,128)S(1)}, f32[128,768]{1,0:T(8,128)S(1)}, u32[]{:S(2)}, u32[]{:S(2)}) collective-permute-start(f32[128,768]{1,0:T(8,128)S(1)} %get-tuple-element.482.refs_0_), channel_id=1, source_target_pairs={{8,0},{12,4},{16,24},{20,28},{9,1},{13,5},{17,25},{21,29},{10,2},{... | collective-permute-start | bytes 1179656 | tf_op jit(solution)/shard_map/ppermute | solution.py:38
  182.2 19.8 %collective-permute-start.88 = (f32[200,768]{1,0:T(8,128)S(1)}, f32[200,768]{1,0:T(8,128)S(1)}, u32[]{:S(2)}, u32[]{:S(2)}) collective-permute-start(f32[200,768]{1,0:T(8,128)S(1)} %get-tuple-element.478.refs_0_), channel_id=1, source_target_pairs={{0,4},{4,0},{8,12},{12,8},{16,20},{20,16},{24,28},{28,24},{1,5},{5... | collective-permute-start | bytes 1843208 | tf_op jit(solution)/shard_map/ppermute | solution.py:34
  183.2 21.2 %collective-permute-start.94 = (f32[128,768]{1,0:T(8,128)S(1)}, f32[128,768]{1,0:T(8,128)S(1)}, u32[]{:S(2)}, u32[]{:S(2)}) collective-permute-start(f32[128,768]{1,0:T(8,128)S(1)} %get-tuple-element.499.refs_0_), channel_id=1, source_target_pairs={{8,0},{12,4},{16,24},{20,28},{9,1},{13,5},{17,25},{21,29},{10,2},{... | collective-permute-start | bytes 1179656 | tf_op jit(solution)/shard_map/ppermute | solution.py:38
  195.3 16.6 %collective-permute-start.95 = (f32[128,768]{1,0:T(8,128)S(1)}, f32[128,768]{1,0:T(8,128)S(1)}, u32[]{:S(2)}, u32[]{:S(2)}) collective-permute-start(f32[128,768]{1,0:T(8,128)S(1)} %collective-permute-done.93.refs_1_), channel_id=1, source_target_pairs={{8,0},{12,4},{16,24},{20,28},{9,1},{13,5},{17,25},{21,29},{10,2},{... | collective-permute-start | bytes 1179656 | tf_op jit(solution)/shard_map/ppermute | solution.py:38
  196.6 16.2 %collective-permute-start.92 = (f32[128,768]{1,0:T(8,128)S(1)}, f32[128,768]{1,0:T(8,128)S(1)}, u32[]{:S(2)}, u32[]{:S(2)}) collective-permute-start(f32[128,768]{1,0:T(8,128)S(1)} %get-tuple-element.498.refs_0_), channel_id=1, source_target_pairs={{0,4},{4,0},{8,12},{12,8},{16,20},{20,16},{24,28},{28,24},{1,5},{5... | collective-permute-start | bytes 1179656 | tf_op jit(solution)/shard_map/ppermute | solution.py:34
  (86 other events, 385.1 us)
where the time goes:
time: 215 us; the launch traced here: 214 us
  waiting for transfers between devices  93.9 us (44%)
  starting transfers between devices  80.8 us (38%)
  Pallas kernels  35.5 us (17%)
    ppermute x24, starting transfers between devices, hop(): return lax.ppermute(a, 'dp', pairs)  43 us
    ppermute x12, waiting for transfers between devices, x_swap(): return lax.ppermute(a, 'dp', swap_pairs(lax.axis_size('dp'), 1))  38.3 us
    pallas_call x67, Pallas kernels, __call__(): pl.pallas_call(kernel, name=getattr(body, 'func', body).__name__, in_spec...  34.9 us
    ppermute x24, waiting for transfers between devices, hop(): return lax.ppermute(a, 'dp', pairs)  30.3 us
    ppermute x12, starting transfers between devices, x_swap(): return lax.ppermute(a, 'dp', swap_pairs(lax.axis_size('dp'), 1))  13.2 us
    ppermute x52, waiting for transfers between devices, core_swap(): return lax.ppermute(a, 'tensor', swap_pairs(lax.axis_size('tensor'), 1))  13.1 us
    ppermute x52, starting transfers between devices, core_swap(): return lax.ppermute(a, 'tensor', swap_pairs(lax.axis_size('tensor'), 1))  12.6 us
    ppermute x8, waiting for transfers between devices, chip_swap(): return lax.ppermute(a, 'tensor', swap_pairs(lax.axis_size('tensor'), 2))  12.2 us
  transfers between devices with their start and end apart: 96, of which 60 were waited for; matrix products, arithmetic and copies ran while one was open for 0% of the time, Pallas kernels for 15%

commit v1 on v0

--- a/solution.py
+++ b/solution.py
@@ -16,6 +16,7 @@
 MIDDLE = [(2, 4), (3, 5), (4, 2), (5, 3)]
 OUTWARD = [(2, 0), (3, 1), (4, 6), (5, 7)]
 CENTRE_X = [(2, 3), (3, 2), (4, 5), (5, 4)]
+OUTER_X = [(0, 1), (1, 0), (6, 7), (7, 6)]
 
 
 def swap_pairs(n, bit):
@@ -461,6 +462,11 @@
         lay(x_bit() == 0, parts[0], parts[1])
         lay(x_bit() != 0, parts[1], parts[0])
         return
+    if kind == "V":
+        for here, far in ((in_centre(), parts[2]), (jnp.logical_not(in_centre()), parts[1])):
+            lay(here & (x_bit() == 0), parts[0], far)
+            lay(here & (x_bit() != 0), far, parts[0])
+        return
     for here, one, two in ((in_centre(), *parts[:2]), (jnp.logical_not(in_centre()), *parts[2:])):
         lay(here & (centre_half() == 0), one, two)
         lay(here & (centre_half() == 1), two, one)
@@ -504,7 +510,7 @@
         lay(far, final)
 
 
-CHUNKS = [("X", 0, 2), ("X", 2, 3), ("X", 3, 4), ("X", 4, 5), ("Z", 5, 6)]
+CHUNKS = [("X", 0, 2), ("V", 2, 4), ("X", 4, 5), ("Z", 5, 6)]
 
 
 class TensorSum:
@@ -556,6 +562,17 @@
         else:
             self.mine = others(self.mine, 2)
         self.parts = [self.mine, x_swap(self.mine)]
+
+
+class XOuter(XFirst):
+    def ch(self):
+        if not on_line_of_four():
+            super().ch()
+            self.parts.append(self.parts[1])
+            return
+        (self.mine,) = self.run(choose, [shape(self.mine.shape)], [self.mine, self.got])
+        other = hop(self.mine, OUTER_X)
+        self.parts = [self.mine, other, hop(other, INWARD)]
 
 
 class ZFirst:
@@ -723,15 +740,15 @@
 
     def ffn_chunk(kind, lo, hi):
         def make():
-            outs = [shape((hi - lo, width))] * 2 if kind == "X" else [shape((2, hi - lo, width))]
+            outs = [shape((2, hi - lo, width))] if kind == "Z" else [shape((hi - lo, width))] * 2
             ins = [r0.act, r1.act, r0.g_ffn, r1.g_ffn, r0.y_low, r1.y_low, r0.g_inner, r1.g_inner]
             return run(functools.partial(ffn_weights, kind, lo, hi), outs, ins)
 
-        return (XFirst if kind == "X" else ZFirst)(run, make)
+        return {"X": XFirst, "V": XOuter, "Z": ZFirst}[kind](run, make)
 
     cuts = [(kind, lo * width // 6, hi * width // 6) for kind, lo, hi in CHUNKS]
     chunks = [ffn_chunk(*cut) for cut in cuts]
-    x, z = ([chunk for chunk in chunks if isinstance(chunk, kind)] for kind in (XFirst, ZFirst))
+    x, v, z = ([chunk for chunk in chunks if type(chunk) is kind] for kind in (XFirst, XOuter, ZFirst))
 
     def attn_one():
         ins = [tokens, r0.gq, r1.gq, r0.gv, r1.gv, r0.pooled, r1.pooled]
@@ -782,58 +799,52 @@
     r0.back.add()
     r1.ffn.tot()
     r1.turn()
-    x[1].make()
+    v[0].make()
     z[0].make()
-    x[2].make()
+    x[0].make()
+    r0.back.tot()
+    r0.aback()
     r1.back.add()
-    r0.back.tot()
-    x[0].make()
-    x[1].xa()
-    r0.aback()
-    x[2].xa()
+    v[0].xa()
     r1.back.tot()
     z[0].ia()
     r1.aback()
+    r0.tok.add()
     a[0].make()
-    x[2].ia()
+    x[0].xa()
     z[0].ma()
-    r0.tok.add()
-    x[0].xa()
-    x[1].ia()
-    x[2].ma()
+    v[0].ia()
     a[1].make()
-    x[1].ma()
+    x[1].make()
+    r0.tok.tot()
     a[0].xa()
-    x[2].ch()
+    r1.tok.add()
     x[0].ia()
-    x[3].make()
-    r0.tok.tot()
+    v[0].ma()
     a[1].xa()
     a[0].ia()
-    x[3].xa()
-    r1.tok.add()
+    r1.tok.tot()
     x[0].ma()
-    x[1].ch()
+    x[1].xa()
+    v[0].ch()
     a[1].ia()
+    a[0].ma()
     z[0].xa()
-    a[0].ma()
-    end(x[2])
+    x[1].ia()
     x[0].ch()
-    r0.tokend()
-    end(x[1])
     a[1].ma()
     a[0].ch()
-    x[3].ia()
     end(x[0])
+    r0.tokend()
+    x[1].ma()
+    end(v[0])
     a[1].ch()
-    r1.tok.tot()
-    x[3].ma()
-    x[3].ch()
+    x[1].ch()
     grad_w_query, grad_w_value = aend0()
     grad_w_key, grad_w_out, grad_b_query, grad_b_value, grad_rel_bias, *small = aend1()
+    end(z[0])
     r1.tokend()
-    end(z[0])
-    end(x[3])
+    end(x[1])
     grad_w_outer, grad_w_inner = Ffn.grads
     grad_b_inner, grad_b_outer, grad_gain_two, grad_shift_two, grad_gain_one, grad_shift_one, grad_b_out = small
     return (

time: 215 us -> 210 us (0.977)
  starting transfers between devices: 80.8 us -> 77.2 us
    ppermute x8, waiting for transfers between devices: 12.2 us -> 23 us  [chip_swap(): return lax.ppermute(a, 'tensor', swap_pairs(lax.axis_size('tensor'), 2))]
    ppermute x12 -> x9, waiting for transfers between devices: 38.3 us -> 27.7 us  [x_swap(): return lax.ppermute(a, 'dp', swap_pairs(lax.axis_size('dp'), 1))]
    ppermute x12 -> x9, starting transfers between devices: 13.2 us -> 6.19 us  [x_swap(): return lax.ppermute(a, 'dp', swap_pairs(lax.axis_size('dp'), 1))]
    ppermute x24 -> x23, starting transfers between devices: 43 us -> 44.7 us  [hop(): return lax.ppermute(a, 'dp', pairs)]
    ppermute x24 -> x23, waiting for transfers between devices: 30.3 us -> 31.7 us  [hop(): return lax.ppermute(a, 'dp', pairs)]
    pallas_call x67 -> x61, Pallas kernels: 34.9 us -> 34.1 us  [__call__(): pl.pallas_call(kernel, name=getattr(body, 'func', body).__name__, in_spec...]
  transfers between devices with their start and end apart: 96 -> 92, of which waited for: 60 -> 59; matrix products, arithmetic and copies ran while one was open for 0% -> 0% of each run, Pallas kernels for 15% -> 15%
where the time goes in v1:
time: 210 us
  waiting for transfers between devices  94.3 us (45%)
  starting transfers between devices  77.2 us (37%)
  Pallas kernels  34.7 us (17%)
    ppermute x23, starting transfers between devices, hop(): return lax.ppermute(a, 'dp', pairs)  44.7 us
    pallas_call x61, Pallas kernels, __call__(): pl.pallas_call(kernel, name=getattr(body, 'func', body).__name__, in_spec...  34.1 us
    ppermute x23, waiting for transfers between devices, hop(): return lax.ppermute(a, 'dp', pairs)  31.7 us
    ppermute x9, waiting for transfers between devices, x_swap(): return lax.ppermute(a, 'dp', swap_pairs(lax.axis_size('dp'), 1))  27.7 us
    ppermute x8, waiting for transfers between devices, chip_swap(): return lax.ppermute(a, 'tensor', swap_pairs(lax.axis_size('tensor'), 2))  23 us
    ppermute x8, starting transfers between devices, chip_swap(): return lax.ppermute(a, 'tensor', swap_pairs(lax.axis_size('tensor'), 2))  13.4 us
    ppermute x52, starting transfers between devices, core_swap(): return lax.ppermute(a, 'tensor', swap_pairs(lax.axis_size('tensor'), 1))  12.9 us
    ppermute x52, waiting for transfers between devices, core_swap(): return lax.ppermute(a, 'tensor', swap_pairs(lax.axis_size('tensor'), 1))  11.9 us
  transfers between devices with their start and end apart: 92, of which 59 were waited for; matrix products, arithmetic and copies ran while one was open for 0% of the time, Pallas kernels for 15%

profile of v1, /device:TPU:0, one launch (start us, length us, event | category | flops | bytes accessed | tf_op | source)
XLA Modules:
  0.0 209.8 jit_solution(759211696128244203)
XLA Ops:
  3.1 2.3 %attend.2 = (bf16[256,192]{1,0:T(8,128)(2,1)S(1)}, bf16[256,192]{1,0:T(8,128)(2,1)S(1)}, bf16[512,192]{1,0:T(8,128)(2,1)S(1)}, bf16[512,192]{1,0:T(8,128)(2,1)S(...) custom-call(s32[2]{0:T(128)S(1)} %copy-done.21, ...), custom_call_target="tpu_custom_call" | custom-call | flops 1024 | bytes 1024 | tf_op jit(solution)/shard_map/attend/pallas_call | solution.py:115
  8.0 2.7 %collective-permute-start.9 = (f32[128,768]{1,0:T(8,128)S(1)}, f32[128,768]{1,0:T(8,128)S(1)}, u32[]{:S(2)}, u32[]{:S(2)}) collective-permute-start(f32[128,768]{1,0:T(8,128)S(1)} %get-tuple-element.267.refs_0_), channel_id=1, source_target_pairs={{0,2},{1,3},{2,0},{3,1},{4,6},{5,7},{6,4},{7,5},{8,10},{9,11},{10,... | collective-permute-start | bytes 1179656 | tf_op jit(solution)/shard_map/ppermute | solution.py:31
  10.7 2.3 %attend.3 = (bf16[256,192]{1,0:T(8,128)(2,1)S(1)}, bf16[256,192]{1,0:T(8,128)(2,1)S(1)}, bf16[512,192]{1,0:T(8,128)(2,1)S(1)}, bf16[512,192]{1,0:T(8,128)(2,1)S(...) custom-call(s32[2]{0:T(128)S(1)} %copy-done.21, ...), custom_call_target="tpu_custom_call" | custom-call | flops 1024 | bytes 1024 | tf_op jit(solution)/shard_map/attend/pallas_call | solution.py:115
  15.4 5.2 %collective-permute-done.9.refs_1_ = f32[128,768]{1,0:T(8,128)S(1)} collective-permute-done((f32[128,768]{1,0:T(8,128)S(1)}, f32[128,768]{1,0:T(8,128)S(1)}, u32[]{:S(2)}, u32[]{:S(2)}) %collective-permute-start.9) | collective-permute-done | bytes 393248 | tf_op jit(solution)/shard_map/ppermute | solution.py:31
  26.5 2.0 collective-permute-start.27
  36.4 2.1 %collective-permute-done.27.refs_1_ = f32[128,768]{1,0:T(8,128)S(1)} collective-permute-done((f32[128,768]{1,0:T(8,128)S(1)}, f32[128,768]{1,0:T(8,128)S(1)}, u32[]{:S(2)}, u32[]{:S(2)}) %collective-permute-start.27) | collective-permute-done | bytes 393248 | tf_op jit(solution)/shard_map/ppermute | solution.py:31
  40.6 2.0 turn.2
  49.3 2.0 turn.3
  53.9 3.5 %collective-permute-start.55 = (f32[2,128,768]{2,1,0:T(8,128)S(1)}, f32[2,128,768]{2,1,0:T(8,128)S(1)}, u32[]{:S(2)}, u32[]{:S(2)}) collective-permute-start(f32[2,128,768]{2,1,0:T(8,128)S(1)} %get-tuple-element.363.refs_0_), channel_id=1, source_target_pairs={{0,8},{4,12},{24,16},{28,20},{1,9},{5,13},{25,17},{29,21},{2,10},{... | collective-permute-start | bytes 2359304 | tf_op jit(solution)/shard_map/ppermute | solution.py:39
  61.5 3.3 %attend_back.2 = (f32[256,768]{1,0:T(8,128)S(1)}, bf16[256,768]{1,0:T(8,128)(2,1)S(1)}, bf16[3,256,512]{2,1,0:T(8,128)(2,1)S(1)}, bf16[256,192]{1,0:T(8,128)(2,1...) custom-call(f32[768]{0:T(1024)S(1)} %copy-done.8, ...), custom_call_target="tpu_custom_call" | custom-call | flops 1024 | bytes 1024 | tf_op jit(solution)/shard_map/attend_back/pallas_call | solution.py:115
  68.7 3.8 %collective-permute-done.50.refs_1_ = f32[256,768]{1,0:T(8,128)S(1)} collective-permute-done((f32[256,768]{1,0:T(8,128)S(1)}, f32[256,768]{1,0:T(8,128)S(1)}, u32[]{:S(2)}, u32[]{:S(2)}) %collective-permute-start.50) | collective-permute-done | bytes 786464 | tf_op jit(solution)/shard_map/ppermute | solution.py:35
  72.6 3.5 %collective-permute-start.60 = (f32[256,768]{1,0:T(8,128)S(1)}, f32[256,768]{1,0:T(8,128)S(1)}, u32[]{:S(2)}, u32[]{:S(2)}) collective-permute-start(f32[256,768]{1,0:T(8,128)S(1)} %get-tuple-element.392.refs_0_), channel_id=1, source_target_pairs={{0,8},{4,12},{24,16},{28,20},{1,9},{5,13},{25,17},{29,21},{2,10},{... | collective-permute-start | bytes 2359304 | tf_op jit(solution)/shard_map/ppermute | solution.py:39
  82.0 3.3 %attend_back.3 = (f32[256,768]{1,0:T(8,128)S(1)}, bf16[256,768]{1,0:T(8,128)(2,1)S(1)}, bf16[3,256,512]{2,1,0:T(8,128)(2,1)S(1)}, bf16[256,192]{1,0:T(8,128)(2,1...) custom-call(f32[768]{0:T(1024)S(1)} %copy-done.8, ...), custom_call_target="tpu_custom_call" | custom-call | flops 1024 | bytes 1024 | tf_op jit(solution)/shard_map/attend_back/pallas_call | solution.py:115
  88.2 5.9 %collective-permute-start.67 = (f32[256,768]{1,0:T(8,128)S(1)}, f32[256,768]{1,0:T(8,128)S(1)}, u32[]{:S(2)}, u32[]{:S(2)}) collective-permute-start(f32[256,768]{1,0:T(8,128)S(1)} %get-tuple-element.410.refs_0_), channel_id=1, source_target_pairs={{0,8},{4,12},{24,16},{28,20},{1,9},{5,13},{25,17},{29,21},{2,10},{... | collective-permute-start | bytes 2359304 | tf_op jit(solution)/shard_map/ppermute | solution.py:39
  97.3 8.0 %collective-permute-done.59.refs_1_ = f32[256,768]{1,0:T(8,128)S(1)} collective-permute-done((f32[256,768]{1,0:T(8,128)S(1)}, f32[256,768]{1,0:T(8,128)S(1)}, u32[]{:S(2)}, u32[]{:S(2)}) %collective-permute-start.59) | collective-permute-done | bytes 786464 | tf_op jit(solution)/shard_map/ppermute | solution.py:31
  106.1 4.3 %collective-permute-done.58.refs_1_ = f32[192,768]{1,0:T(8,128)S(1)} collective-permute-done((f32[192,768]{1,0:T(8,128)S(1)}, f32[192,768]{1,0:T(8,128)S(1)}, u32[]{:S(2)}, u32[]{:S(2)}) %collective-permute-start.58) | collective-permute-done | bytes 589856 | tf_op jit(solution)/shard_map/ppermute | solution.py:35
  110.5 2.1 collective-permute-start.64
  116.5 6.3 %collective-permute-done.65.refs_1_ = f32[200,768]{1,0:T(8,128)S(1)} collective-permute-done((f32[200,768]{1,0:T(8,128)S(1)}, f32[200,768]{1,0:T(8,128)S(1)}, u32[]{:S(2)}, u32[]{:S(2)}) %collective-permute-start.65) | collective-permute-done | bytes 614432 | tf_op jit(solution)/shard_map/ppermute | solution.py:35
  123.0 3.7 %collective-permute-start.76 = (f32[200,768]{1,0:T(8,128)S(1)}, f32[200,768]{1,0:T(8,128)S(1)}, u32[]{:S(2)}, u32[]{:S(2)}) collective-permute-start(f32[200,768]{1,0:T(8,128)S(1)} %get-tuple-element.428.refs_0_), channel_id=1, source_target_pairs={{0,8},{4,12},{24,16},{28,20},{1,9},{5,13},{25,17},{29,21},{2,10},{... | collective-permute-start | bytes 1843208 | tf_op jit(solution)/shard_map/ppermute | solution.py:39
  127.3 3.7 %collective-permute-done.63.refs_1_ = f32[256,768]{1,0:T(8,128)S(1)} collective-permute-done((f32[256,768]{1,0:T(8,128)S(1)}, f32[256,768]{1,0:T(8,128)S(1)}, u32[]{:S(2)}, u32[]{:S(2)}) %collective-permute-start.63) | collective-permute-done | bytes 786464 | tf_op jit(solution)/shard_map/ppermute | solution.py:31
  133.2 2.7 %collective-permute-done.72.refs_1_ = f32[128,768]{1,0:T(8,128)S(1)} collective-permute-done((f32[128,768]{1,0:T(8,128)S(1)}, f32[128,768]{1,0:T(8,128)S(1)}, u32[]{:S(2)}, u32[]{:S(2)}) %collective-permute-start.72) | collective-permute-done | bytes 393248 | tf_op jit(solution)/shard_map/ppermute | solution.py:35
  136.0 2.7 %collective-permute-start.84 = (f32[256,768]{1,0:T(8,128)S(1)}, f32[256,768]{1,0:T(8,128)S(1)}, u32[]{:S(2)}, u32[]{:S(2)}) collective-permute-start(f32[256,768]{1,0:T(8,128)S(1)} %get-tuple-element.445.refs_0_), channel_id=1, source_target_pairs={{0,4},{4,0},{24,28},{28,24},{1,5},{5,1},{25,29},{29,25},{2,6},{6,2... | collective-permute-start | bytes 2359304 | tf_op jit(solution)/shard_map/ppermute | solution.py:39
  139.5 4.8 %collective-permute-start.73 = (f32[128,768]{1,0:T(8,128)S(1)}, f32[128,768]{1,0:T(8,128)S(1)}, u32[]{:S(2)}, u32[]{:S(2)}) collective-permute-start(f32[128,768]{1,0:T(8,128)S(1)} %get-tuple-element.425.refs_0_), channel_id=1, source_target_pairs={{0,8},{4,12},{24,16},{28,20},{1,9},{5,13},{25,17},{29,21},{2,10},{... | collective-permute-start | bytes 1179656 | tf_op jit(solution)/shard_map/ppermute | solution.py:39
  146.5 4.3 %collective-permute-done.73.refs_1_ = f32[128,768]{1,0:T(8,128)S(1)} collective-permute-done((f32[128,768]{1,0:T(8,128)S(1)}, f32[128,768]{1,0:T(8,128)S(1)}, u32[]{:S(2)}, u32[]{:S(2)}) %collective-permute-start.73) | collective-permute-done | bytes 393248 | tf_op jit(solution)/shard_map/ppermute | solution.py:39
  150.9 2.3 %collective-permute-done.71.refs_1_ = f32[256,768]{1,0:T(8,128)S(1)} collective-permute-done((f32[256,768]{1,0:T(8,128)S(1)}, f32[256,768]{1,0:T(8,128)S(1)}, u32[]{:S(2)}, u32[]{:S(2)}) %collective-permute-start.71) | collective-permute-done | bytes 786464 | tf_op jit(solution)/shard_map/ppermute | solution.py:39
  155.1 3.6 %collective-permute-start.85 = (f32[256,768]{1,0:T(8,128)S(1)}, f32[256,768]{1,0:T(8,128)S(1)}, u32[]{:S(2)}, u32[]{:S(2)}) collective-permute-start(f32[256,768]{1,0:T(8,128)S(1)} %collective-permute-done.84.refs_1_), channel_id=1, source_target_pairs={{0,8},{4,12},{24,16},{28,20},{1,9},{5,13},{25,17},{29,21},{2,10},{... | collective-permute-start | bytes 2359304 | tf_op jit(solution)/shard_map/ppermute | solution.py:39
  160.1 7.3 %collective-permute-done.79.refs_1_ = f32[192,768]{1,0:T(8,128)S(1)} collective-permute-done((f32[192,768]{1,0:T(8,128)S(1)}, f32[192,768]{1,0:T(8,128)S(1)}, u32[]{:S(2)}, u32[]{:S(2)}) %collective-permute-start.79) | collective-permute-done | bytes 589856 | tf_op jit(solution)/shard_map/ppermute | solution.py:39
  168.2 3.3 %collective-permute-done.78.refs_1_ = f32[256,768]{1,0:T(8,128)S(1)} collective-permute-done((f32[256,768]{1,0:T(8,128)S(1)}, f32[256,768]{1,0:T(8,128)S(1)}, u32[]{:S(2)}, u32[]{:S(2)}) %collective-permute-start.78) | collective-permute-done | bytes 786464 | tf_op jit(solution)/shard_map/ppermute | solution.py:35
  178.2 4.4 %collective-permute-done.87.refs_1_ = f32[200,768]{1,0:T(8,128)S(1)} collective-permute-done((f32[200,768]{1,0:T(8,128)S(1)}, f32[200,768]{1,0:T(8,128)S(1)}, u32[]{:S(2)}, u32[]{:S(2)}) %collective-permute-start.87) | collective-permute-done | bytes 614432 | tf_op jit(solution)/shard_map/ppermute | solution.py:39
  184.0 7.3 %collective-permute-done.90.refs_1_ = f32[128,768]{1,0:T(8,128)S(1)} collective-permute-done((f32[128,768]{1,0:T(8,128)S(1)}, f32[128,768]{1,0:T(8,128)S(1)}, u32[]{:S(2)}, u32[]{:S(2)}) %collective-permute-start.90) | collective-permute-done | bytes 393248 | tf_op jit(solution)/shard_map/ppermute | solution.py:39
  193.8 7.0 %collective-permute-done.88.refs_1_ = f32[200,768]{1,0:T(8,128)S(1)} collective-permute-done((f32[200,768]{1,0:T(8,128)S(1)}, f32[200,768]{1,0:T(8,128)S(1)}, u32[]{:S(2)}, u32[]{:S(2)}) %collective-permute-start.88) | collective-permute-done | bytes 614432 | tf_op jit(solution)/shard_map/ppermute | solution.py:35
  202.0 4.5 %collective-permute-done.83.refs_3_ = f32[128,768]{1,0:T(8,128)S(1)} collective-permute-done((f32[128,768]{1,0:T(8,128)S(1)}, f32[128,768]{1,0:T(8,128)S(1)}, u32[]{:S(2)}, u32[]{:S(2)}) %collective-permute-start.83) | collective-permute-done | bytes 393248 | tf_op jit(solution)/shard_map/ppermute | solution.py:39
  (258 shorter events, 81.5 us)
Async XLA Ops:
  52.0 20.5 %collective-permute-start.50 = (f32[256,768]{1,0:T(8,128)S(1)}, f32[256,768]{1,0:T(8,128)S(1)}, u32[]{:S(2)}, u32[]{:S(2)}) collective-permute-start(f32[256,768]{1,0:T(8,128)S(1)} %get-tuple-element.356), channel_id=1, source_target_pairs={{0,4},{4,0},{8,12},{12,8},{16,20},{20,16},{24,28},{28,24},{1,5},{5... | collective-permute-start | bytes 2359304 | tf_op jit(solution)/shard_map/ppermute | solution.py:35
  53.9 24.2 %collective-permute-start.55 = (f32[2,128,768]{2,1,0:T(8,128)S(1)}, f32[2,128,768]{2,1,0:T(8,128)S(1)}, u32[]{:S(2)}, u32[]{:S(2)}) collective-permute-start(f32[2,128,768]{2,1,0:T(8,128)S(1)} %get-tuple-element.363.refs_0_), channel_id=1, source_target_pairs={{0,8},{4,12},{24,16},{28,20},{1,9},{5,13},{25,17},{29,21},{2,10},{... | collective-permute-start | bytes 2359304 | tf_op jit(solution)/shard_map/ppermute | solution.py:39
  64.9 20.5 %collective-permute-start.57 = (f32[256,768]{1,0:T(8,128)S(1)}, f32[256,768]{1,0:T(8,128)S(1)}, u32[]{:S(2)}, u32[]{:S(2)}) collective-permute-start(f32[256,768]{1,0:T(8,128)S(1)} %get-tuple-element.374), channel_id=1, source_target_pairs={{0,1},{1,0},{2,3},{3,2},{4,5},{5,4},{6,7},{7,6},{8,9},{9,8},{10,11... | collective-permute-start | bytes 2359304 | tf_op jit(solution)/shard_map/ppermute | solution.py:27
  65.3 22.8 %collective-permute-start.62 = (f32[256,768]{1,0:T(8,128)S(1)}, f32[256,768]{1,0:T(8,128)S(1)}, u32[]{:S(2)}, u32[]{:S(2)}) collective-permute-start(f32[256,768]{1,0:T(8,128)S(1)} %get-tuple-element.396), channel_id=1, source_target_pairs={{0,4},{4,0},{8,12},{12,8},{16,20},{20,16},{24,28},{28,24},{1,5},{5... | collective-permute-start | bytes 2359304 | tf_op jit(solution)/shard_map/ppermute | solution.py:35
  72.6 22.2 %collective-permute-start.60 = (f32[256,768]{1,0:T(8,128)S(1)}, f32[256,768]{1,0:T(8,128)S(1)}, u32[]{:S(2)}, u32[]{:S(2)}) collective-permute-start(f32[256,768]{1,0:T(8,128)S(1)} %get-tuple-element.392.refs_0_), channel_id=1, source_target_pairs={{0,8},{4,12},{24,16},{28,20},{1,9},{5,13},{25,17},{29,21},{2,10},{... | collective-permute-start | bytes 2359304 | tf_op jit(solution)/shard_map/ppermute | solution.py:39
  79.7 14.5 %collective-permute-start.61 = (f32[128,768]{1,0:T(8,128)S(1)}, f32[128,768]{1,0:T(8,128)S(1)}, u32[]{:S(2)}, u32[]{:S(2)}) collective-permute-start(f32[128,768]{1,0:T(8,128)S(1)} %get-tuple-element.394), channel_id=1, source_target_pairs={{8,16},{12,20},{16,8},{20,12},{9,17},{13,21},{17,9},{21,13},{10,18... | collective-permute-start | bytes 1179656 | tf_op jit(solution)/shard_map/ppermute | solution.py:39
  85.5 19.8 %collective-permute-start.59 = (f32[256,768]{1,0:T(8,128)S(1)}, f32[256,768]{1,0:T(8,128)S(1)}, u32[]{:S(2)}, u32[]{:S(2)}) collective-permute-start(f32[256,768]{1,0:T(8,128)S(1)} %get-tuple-element.379.refs_0_), channel_id=1, source_target_pairs={{0,2},{1,3},{2,0},{3,1},{4,6},{5,7},{6,4},{7,5},{8,10},{9,11},{10,... | collective-permute-start | bytes 2359304 | tf_op jit(solution)/shard_map/ppermute | solution.py:31
  87.1 25.5 %collective-permute-start.56 = (f32[256,768]{1,0:T(8,128)S(1)}, f32[256,768]{1,0:T(8,128)S(1)}, u32[]{:S(2)}, u32[]{:S(2)}) collective-permute-start(f32[256,768]{1,0:T(8,128)S(1)} %get-tuple-element.368), channel_id=1, source_target_pairs={{0,1},{1,0},{2,3},{3,2},{4,5},{5,4},{6,7},{7,6},{8,9},{9,8},{10,11... | collective-permute-start | bytes 2359304 | tf_op jit(solution)/shard_map/ppermute | solution.py:27
  88.2 26.1 %collective-permute-start.67 = (f32[256,768]{1,0:T(8,128)S(1)}, f32[256,768]{1,0:T(8,128)S(1)}, u32[]{:S(2)}, u32[]{:S(2)}) collective-permute-start(f32[256,768]{1,0:T(8,128)S(1)} %get-tuple-element.410.refs_0_), channel_id=1, source_target_pairs={{0,8},{4,12},{24,16},{28,20},{1,9},{5,13},{25,17},{29,21},{2,10},{... | collective-permute-start | bytes 2359304 | tf_op jit(solution)/shard_map/ppermute | solution.py:39
  94.2 16.2 %collective-permute-start.58 = (f32[192,768]{1,0:T(8,128)S(1)}, f32[192,768]{1,0:T(8,128)S(1)}, u32[]{:S(2)}, u32[]{:S(2)}) collective-permute-start(f32[192,768]{1,0:T(8,128)S(1)} %get-tuple-element.378), channel_id=1, source_target_pairs={{0,4},{4,0},{8,12},{12,8},{16,20},{20,16},{24,28},{28,24},{1,5},{5... | collective-permute-start | bytes 1769480 | tf_op jit(solution)/shard_map/ppermute | solution.py:35
  94.9 20.2 %collective-permute-start.66 = (f32[256,768]{1,0:T(8,128)S(1)}, f32[256,768]{1,0:T(8,128)S(1)}, u32[]{:S(2)}, u32[]{:S(2)}) collective-permute-start(f32[256,768]{1,0:T(8,128)S(1)} %get-tuple-element.409.refs_0_), channel_id=1, source_target_pairs={{8,16},{12,20},{16,8},{20,12},{9,17},{13,21},{17,9},{21,13},{10,18... | collective-permute-start | bytes 2359304 | tf_op jit(solution)/shard_map/ppermute | solution.py:39
  105.3 17.6 %collective-permute-start.65 = (f32[200,768]{1,0:T(8,128)S(1)}, f32[200,768]{1,0:T(8,128)S(1)}, u32[]{:S(2)}, u32[]{:S(2)}) collective-permute-start(f32[200,768]{1,0:T(8,128)S(1)} %get-tuple-element.408), channel_id=1, source_target_pairs={{0,4},{4,0},{8,12},{12,8},{16,20},{20,16},{24,28},{28,24},{1,5},{5... | collective-permute-start | bytes 1843208 | tf_op jit(solution)/shard_map/ppermute | solution.py:35
  110.5 16.2 %collective-permute-start.64 = (f32[192,768]{1,0:T(8,128)S(1)}, f32[192,768]{1,0:T(8,128)S(1)}, u32[]{:S(2)}, u32[]{:S(2)}) collective-permute-start(f32[192,768]{1,0:T(8,128)S(1)} %get-tuple-element.406.refs_0_), channel_id=1, source_target_pairs={{0,8},{4,12},{24,16},{28,20},{1,9},{5,13},{25,17},{29,21},{2,10},{... | collective-permute-start | bytes 1769480 | tf_op jit(solution)/shard_map/ppermute | solution.py:39
  112.7 18.3 %collective-permute-start.63 = (f32[256,768]{1,0:T(8,128)S(1)}, f32[256,768]{1,0:T(8,128)S(1)}, u32[]{:S(2)}, u32[]{:S(2)}) collective-permute-start(f32[256,768]{1,0:T(8,128)S(1)} %get-tuple-element.405.refs_0_), channel_id=1, source_target_pairs={{0,2},{1,3},{2,0},{3,1},{4,6},{5,7},{6,4},{7,5},{8,10},{9,11},{10,... | collective-permute-start | bytes 2359304 | tf_op jit(solution)/shard_map/ppermute | solution.py:31
  114.4 16.7 %collective-permute-start.70 = (f32[256,768]{1,0:T(8,128)S(1)}, f32[256,768]{1,0:T(8,128)S(1)}, u32[]{:S(2)}, u32[]{:S(2)}) collective-permute-start(f32[256,768]{1,0:T(8,128)S(1)} %get-tuple-element.419.refs_0_), channel_id=1, source_target_pairs={{8,16},{12,20},{16,8},{20,12},{9,17},{13,21},{17,9},{21,13},{10,18... | collective-permute-start | bytes 2359304 | tf_op jit(solution)/shard_map/ppermute | solution.py:39
  115.2 20.7 %collective-permute-start.77 = (f32[256,768]{1,0:T(8,128)S(1)}, f32[256,768]{1,0:T(8,128)S(1)}, u32[]{:S(2)}, u32[]{:S(2)}) collective-permute-start(f32[256,768]{1,0:T(8,128)S(1)} %get-tuple-element.429.refs_0_), channel_id=1, source_target_pairs={{8,0},{12,4},{16,24},{20,28},{9,1},{13,5},{17,25},{21,29},{10,2},{... | collective-permute-start | bytes 2359304 | tf_op jit(solution)/shard_map/ppermute | solution.py:39
  123.0 16.5 %collective-permute-start.76 = (f32[200,768]{1,0:T(8,128)S(1)}, f32[200,768]{1,0:T(8,128)S(1)}, u32[]{:S(2)}, u32[]{:S(2)}) collective-permute-start(f32[200,768]{1,0:T(8,128)S(1)} %get-tuple-element.428.refs_0_), channel_id=1, source_target_pairs={{0,8},{4,12},{24,16},{28,20},{1,9},{5,13},{25,17},{29,21},{2,10},{... | collective-permute-start | bytes 1843208 | tf_op jit(solution)/shard_map/ppermute | solution.py:39
  131.2 21.9 %collective-permute-start.71 = (f32[256,768]{1,0:T(8,128)S(1)}, f32[256,768]{1,0:T(8,128)S(1)}, u32[]{:S(2)}, u32[]{:S(2)}) collective-permute-start(f32[256,768]{1,0:T(8,128)S(1)} %get-tuple-element.421.refs_0_), channel_id=1, source_target_pairs={{8,0},{12,4},{16,24},{20,28},{9,1},{13,5},{17,25},{21,29},{10,2},{... | collective-permute-start | bytes 2359304 | tf_op jit(solution)/shard_map/ppermute | solution.py:39
  136.0 19.1 %collective-permute-start.84 = (f32[256,768]{1,0:T(8,128)S(1)}, f32[256,768]{1,0:T(8,128)S(1)}, u32[]{:S(2)}, u32[]{:S(2)}) collective-permute-start(f32[256,768]{1,0:T(8,128)S(1)} %get-tuple-element.445.refs_0_), channel_id=1, source_target_pairs={{0,4},{4,0},{24,28},{28,24},{1,5},{5,1},{25,29},{29,25},{2,6},{6,2... | collective-permute-start | bytes 2359304 | tf_op jit(solution)/shard_map/ppermute | solution.py:39
  144.4 14.3 %collective-permute-start.80 = (f32[200,768]{1,0:T(8,128)S(1)}, f32[200,768]{1,0:T(8,128)S(1)}, u32[]{:S(2)}, u32[]{:S(2)}) collective-permute-start(f32[200,768]{1,0:T(8,128)S(1)} %get-tuple-element.438.refs_0_), channel_id=1, source_target_pairs={{8,16},{12,20},{16,8},{20,12},{9,17},{13,21},{17,9},{21,13},{10,18... | collective-permute-start | bytes 1843208 | tf_op jit(solution)/shard_map/ppermute | solution.py:39
  145.2 22.3 %collective-permute-start.79 = (f32[192,768]{1,0:T(8,128)S(1)}, f32[192,768]{1,0:T(8,128)S(1)}, u32[]{:S(2)}, u32[]{:S(2)}) collective-permute-start(f32[192,768]{1,0:T(8,128)S(1)} %get-tuple-element.437.refs_0_), channel_id=1, source_target_pairs={{8,0},{12,4},{16,24},{20,28},{9,1},{13,5},{17,25},{21,29},{10,2},{... | collective-permute-start | bytes 1769480 | tf_op jit(solution)/shard_map/ppermute | solution.py:39
  153.2 18.3 %collective-permute-start.78 = (f32[256,768]{1,0:T(8,128)S(1)}, f32[256,768]{1,0:T(8,128)S(1)}, u32[]{:S(2)}, u32[]{:S(2)}) collective-permute-start(f32[256,768]{1,0:T(8,128)S(1)} %get-tuple-element.436.refs_0_), channel_id=1, source_target_pairs={{0,4},{4,0},{8,12},{12,8},{16,20},{20,16},{24,28},{28,24},{1,5},{5... | collective-permute-start | bytes 2359304 | tf_op jit(solution)/shard_map/ppermute | solution.py:35
  153.5 20.0 %collective-permute-start.69 = (f32[256,768]{1,0:T(8,128)S(1)}, f32[256,768]{1,0:T(8,128)S(1)}, u32[]{:S(2)}, u32[]{:S(2)}) collective-permute-start(f32[256,768]{1,0:T(8,128)S(1)} %get-tuple-element.418.refs_1_), channel_id=1, source_target_pairs={{0,1},{1,0},{2,3},{3,2},{4,5},{5,4},{6,7},{7,6},{8,9},{9,8},{10,11... | collective-permute-start | bytes 2359304 | tf_op jit(solution)/shard_map/ppermute | solution.py:27
  155.1 21.8 %collective-permute-start.85 = (f32[256,768]{1,0:T(8,128)S(1)}, f32[256,768]{1,0:T(8,128)S(1)}, u32[]{:S(2)}, u32[]{:S(2)}) collective-permute-start(f32[256,768]{1,0:T(8,128)S(1)} %collective-permute-done.84.refs_1_), channel_id=1, source_target_pairs={{0,8},{4,12},{24,16},{28,20},{1,9},{5,13},{25,17},{29,21},{2,10},{... | collective-permute-start | bytes 2359304 | tf_op jit(solution)/shard_map/ppermute | solution.py:39
  158.8 23.7 %collective-permute-start.87 = (f32[200,768]{1,0:T(8,128)S(1)}, f32[200,768]{1,0:T(8,128)S(1)}, u32[]{:S(2)}, u32[]{:S(2)}) collective-permute-start(f32[200,768]{1,0:T(8,128)S(1)} %get-tuple-element.453.refs_0_), channel_id=1, source_target_pairs={{8,0},{12,4},{16,24},{20,28},{9,1},{13,5},{17,25},{21,29},{10,2},{... | collective-permute-start | bytes 1843208 | tf_op jit(solution)/shard_map/ppermute | solution.py:39
  171.5 21.2 %collective-permute-start.89 = (f32[192,768]{1,0:T(8,128)S(1)}, f32[192,768]{1,0:T(8,128)S(1)}, u32[]{:S(2)}, u32[]{:S(2)}) collective-permute-start(f32[192,768]{1,0:T(8,128)S(1)} %get-tuple-element.456.refs_0_), channel_id=1, source_target_pairs={{0,4},{4,0},{8,12},{12,8},{16,20},{20,16},{24,28},{28,24},{1,5},{5... | collective-permute-start | bytes 1769480 | tf_op jit(solution)/shard_map/ppermute | solution.py:35
  175.6 15.7 %collective-permute-start.90 = (f32[128,768]{1,0:T(8,128)S(1)}, f32[128,768]{1,0:T(8,128)S(1)}, u32[]{:S(2)}, u32[]{:S(2)}) collective-permute-start(f32[128,768]{1,0:T(8,128)S(1)} %get-tuple-element.457.refs_0_), channel_id=1, source_target_pairs={{8,0},{12,4},{16,24},{20,28},{9,1},{13,5},{17,25},{21,29},{10,2},{... | collective-permute-start | bytes 1179656 | tf_op jit(solution)/shard_map/ppermute | solution.py:39
  176.9 30.5 %collective-permute-start.68 = (f32[256,768]{1,0:T(8,128)S(1)}, f32[256,768]{1,0:T(8,128)S(1)}, u32[]{:S(2)}, u32[]{:S(2)}) collective-permute-start(f32[256,768]{1,0:T(8,128)S(1)} %get-tuple-element.416.refs_1_), channel_id=1, source_target_pairs={{0,1},{1,0},{2,3},{3,2},{4,5},{5,4},{6,7},{7,6},{8,9},{9,8},{10,11... | collective-permute-start | bytes 2359304 | tf_op jit(solution)/shard_map/ppermute | solution.py:27
  182.6 18.2 %collective-permute-start.88 = (f32[200,768]{1,0:T(8,128)S(1)}, f32[200,768]{1,0:T(8,128)S(1)}, u32[]{:S(2)}, u32[]{:S(2)}) collective-permute-start(f32[200,768]{1,0:T(8,128)S(1)} %get-tuple-element.455.refs_0_), channel_id=1, source_target_pairs={{0,4},{4,0},{8,12},{12,8},{16,20},{20,16},{24,28},{28,24},{1,5},{5... | collective-permute-start | bytes 1843208 | tf_op jit(solution)/shard_map/ppermute | solution.py:35
  182.7 19.3 %collective-permute-start.82 = (f32[128,768]{1,0:T(8,128)S(1)}, f32[128,768]{1,0:T(8,128)S(1)}, u32[]{:S(2)}, u32[]{:S(2)}) collective-permute-start(f32[128,768]{1,0:T(8,128)S(1)} %get-tuple-element.444.refs_0_), channel_id=1, source_target_pairs={{8,0},{12,4},{16,24},{20,28},{9,1},{13,5},{17,25},{21,29},{10,2},{... | collective-permute-start | bytes 1179656 | tf_op jit(solution)/shard_map/ppermute | solution.py:39
  191.3 15.3 %collective-permute-start.83 = (f32[128,768]{1,0:T(8,128)S(1)}, f32[128,768]{1,0:T(8,128)S(1)}, u32[]{:S(2)}, u32[]{:S(2)}) collective-permute-start(f32[128,768]{1,0:T(8,128)S(1)} %collective-permute-done.81.refs_1_), channel_id=1, source_target_pairs={{8,0},{12,4},{16,24},{20,28},{9,1},{13,5},{17,25},{21,29},{10,2},{... | collective-permute-start | bytes 1179656 | tf_op jit(solution)/shard_map/ppermute | solution.py:39
  192.6 16.1 %collective-permute-start.91 = (f32[128,768]{1,0:T(8,128)S(1)}, f32[128,768]{1,0:T(8,128)S(1)}, u32[]{:S(2)}, u32[]{:S(2)}) collective-permute-start(f32[128,768]{1,0:T(8,128)S(1)} %get-tuple-element.474.refs_0_), channel_id=1, source_target_pairs={{0,4},{4,0},{8,12},{12,8},{16,20},{20,16},{24,28},{28,24},{1,5},{5... | collective-permute-start | bytes 1179656 | tf_op jit(solution)/shard_map/ppermute | solution.py:35
  (82 other events, 353.7 us)

commit v2 on v1

--- a/solution.py
+++ b/solution.py
@@ -834,8 +834,8 @@
     x[0].ch()
     a[1].ma()
     a[0].ch()
+    r0.tokend()
     end(x[0])
-    r0.tokend()
     x[1].ma()
     end(v[0])
     a[1].ch()

time: 210 us -> 207 us (0.986)
  waiting for transfers between devices: 94.3 us -> 86.6 us
  starting transfers between devices: 77.2 us -> 81.5 us
    ppermute x9, starting transfers between devices: 6.19 us -> 13 us  [x_swap(): return lax.ppermute(a, 'dp', swap_pairs(lax.axis_size('dp'), 1))]
    ppermute x23, waiting for transfers between devices: 31.7 us -> 27.5 us  [hop(): return lax.ppermute(a, 'dp', pairs)]
    ppermute x23, starting transfers between devices: 44.7 us -> 41.8 us  [hop(): return lax.ppermute(a, 'dp', pairs)]
    ppermute x8, waiting for transfers between devices: 23 us -> 20.4 us  [chip_swap(): return lax.ppermute(a, 'tensor', swap_pairs(lax.axis_size('tensor'), 2))]
  transfers between devices with their start and end apart: 92 -> 92, of which waited for: 59 -> 58; matrix products, arithmetic and copies ran while one was open for 0% -> 0% of each run, Pallas kernels for 15% -> 15%
where the time goes in v2:
time: 207 us
  waiting for transfers between devices  86.6 us (42%)
  starting transfers between devices  81.5 us (39%)
  Pallas kernels  34.7 us (17%)
    ppermute x23, starting transfers between devices, hop(): return lax.ppermute(a, 'dp', pairs)  41.8 us
    pallas_call x61, Pallas kernels, __call__(): pl.pallas_call(kernel, name=getattr(body, 'func', body).__name__, in_spec...  34.1 us
    ppermute x23, waiting for transfers between devices, hop(): return lax.ppermute(a, 'dp', pairs)  27.5 us
    ppermute x9, waiting for transfers between devices, x_swap(): return lax.ppermute(a, 'dp', swap_pairs(lax.axis_size('dp'), 1))  26.9 us
    ppermute x8, waiting for transfers between devices, chip_swap(): return lax.ppermute(a, 'tensor', swap_pairs(lax.axis_size('tensor'), 2))  20.4 us
    ppermute x8, starting transfers between devices, chip_swap(): return lax.ppermute(a, 'tensor', swap_pairs(lax.axis_size('tensor'), 2))  13.8 us
    ppermute x9, starting transfers between devices, x_swap(): return lax.ppermute(a, 'dp', swap_pairs(lax.axis_size('dp'), 1))  13 us
    ppermute x52, starting transfers between devices, core_swap(): return lax.ppermute(a, 'tensor', swap_pairs(lax.axis_size('tensor'), 1))  12.9 us
  transfers between devices with their start and end apart: 92, of which 58 were waited for; matrix products, arithmetic and copies ran while one was open for 0% of the time, Pallas kernels for 15%

profile of v2, /device:TPU:0, one launch (start us, length us, event | category | flops | bytes accessed | tf_op | source)
XLA Modules:
  0.0 206.5 jit_solution(13601508070885760335)
XLA Ops:
  3.1 2.3 %attend.2 = (bf16[256,192]{1,0:T(8,128)(2,1)S(1)}, bf16[256,192]{1,0:T(8,128)(2,1)S(1)}, bf16[512,192]{1,0:T(8,128)(2,1)S(1)}, bf16[512,192]{1,0:T(8,128)(2,1)S(...) custom-call(s32[2]{0:T(128)S(1)} %copy-done.21, ...), custom_call_target="tpu_custom_call" | custom-call | flops 1024 | bytes 1024 | tf_op jit(solution)/shard_map/attend/pallas_call | solution.py:115
  8.0 2.7 %collective-permute-start.9 = (f32[128,768]{1,0:T(8,128)S(1)}, f32[128,768]{1,0:T(8,128)S(1)}, u32[]{:S(2)}, u32[]{:S(2)}) collective-permute-start(f32[128,768]{1,0:T(8,128)S(1)} %get-tuple-element.267.refs_0_), channel_id=1, source_target_pairs={{0,2},{1,3},{2,0},{3,1},{4,6},{5,7},{6,4},{7,5},{8,10},{9,11},{10,... | collective-permute-start | bytes 1179656 | tf_op jit(solution)/shard_map/ppermute | solution.py:31
  10.7 2.3 %attend.3 = (bf16[256,192]{1,0:T(8,128)(2,1)S(1)}, bf16[256,192]{1,0:T(8,128)(2,1)S(1)}, bf16[512,192]{1,0:T(8,128)(2,1)S(1)}, bf16[512,192]{1,0:T(8,128)(2,1)S(...) custom-call(s32[2]{0:T(128)S(1)} %copy-done.21, ...), custom_call_target="tpu_custom_call" | custom-call | flops 1024 | bytes 1024 | tf_op jit(solution)/shard_map/attend/pallas_call | solution.py:115
  15.4 5.2 %collective-permute-done.9.refs_1_ = f32[128,768]{1,0:T(8,128)S(1)} collective-permute-done((f32[128,768]{1,0:T(8,128)S(1)}, f32[128,768]{1,0:T(8,128)S(1)}, u32[]{:S(2)}, u32[]{:S(2)}) %collective-permute-start.9) | collective-permute-done | bytes 393248 | tf_op jit(solution)/shard_map/ppermute | solution.py:31
  26.5 2.0 collective-permute-start.27
  34.6 1.8 collective-permute-start.26
  36.4 2.1 %collective-permute-done.27.refs_1_ = f32[128,768]{1,0:T(8,128)S(1)} collective-permute-done((f32[128,768]{1,0:T(8,128)S(1)}, f32[128,768]{1,0:T(8,128)S(1)}, u32[]{:S(2)}, u32[]{:S(2)}) %collective-permute-start.27) | collective-permute-done | bytes 393248 | tf_op jit(solution)/shard_map/ppermute | solution.py:31
  40.6 2.0 turn.2
  49.3 2.0 turn.3
  53.9 3.5 %collective-permute-start.55 = (f32[2,128,768]{2,1,0:T(8,128)S(1)}, f32[2,128,768]{2,1,0:T(8,128)S(1)}, u32[]{:S(2)}, u32[]{:S(2)}) collective-permute-start(f32[2,128,768]{2,1,0:T(8,128)S(1)} %get-tuple-element.363.refs_0_), channel_id=1, source_target_pairs={{0,8},{4,12},{24,16},{28,20},{1,9},{5,13},{25,17},{29,21},{2,10},{... | collective-permute-start | bytes 2359304 | tf_op jit(solution)/shard_map/ppermute | solution.py:39
  61.5 3.3 %attend_back.2 = (f32[256,768]{1,0:T(8,128)S(1)}, bf16[256,768]{1,0:T(8,128)(2,1)S(1)}, bf16[3,256,512]{2,1,0:T(8,128)(2,1)S(1)}, bf16[256,192]{1,0:T(8,128)(2,1...) custom-call(f32[768]{0:T(1024)S(1)} %copy-done.8, ...), custom_call_target="tpu_custom_call" | custom-call | flops 1024 | bytes 1024 | tf_op jit(solution)/shard_map/attend_back/pallas_call | solution.py:115
  65.4 1.8 collective-permute-start.49
  68.7 3.8 %collective-permute-done.50.refs_1_ = f32[256,768]{1,0:T(8,128)S(1)} collective-permute-done((f32[256,768]{1,0:T(8,128)S(1)}, f32[256,768]{1,0:T(8,128)S(1)}, u32[]{:S(2)}, u32[]{:S(2)}) %collective-permute-start.50) | collective-permute-done | bytes 786464 | tf_op jit(solution)/shard_map/ppermute | solution.py:35
  72.6 3.5 %collective-permute-start.60 = (f32[256,768]{1,0:T(8,128)S(1)}, f32[256,768]{1,0:T(8,128)S(1)}, u32[]{:S(2)}, u32[]{:S(2)}) collective-permute-start(f32[256,768]{1,0:T(8,128)S(1)} %get-tuple-element.392.refs_0_), channel_id=1, source_target_pairs={{0,8},{4,12},{24,16},{28,20},{1,9},{5,13},{25,17},{29,21},{2,10},{... | collective-permute-start | bytes 2359304 | tf_op jit(solution)/shard_map/ppermute | solution.py:39
  80.6 3.3 %attend_back.3 = (f32[256,768]{1,0:T(8,128)S(1)}, bf16[256,768]{1,0:T(8,128)(2,1)S(1)}, bf16[3,256,512]{2,1,0:T(8,128)(2,1)S(1)}, bf16[256,192]{1,0:T(8,128)(2,1...) custom-call(f32[768]{0:T(1024)S(1)} %copy-done.8, ...), custom_call_target="tpu_custom_call" | custom-call | flops 1024 | bytes 1024 | tf_op jit(solution)/shard_map/attend_back/pallas_call | solution.py:115
  84.0 1.8 collective-permute-start.59
  88.2 4.7 %collective-permute-start.67 = (f32[256,768]{1,0:T(8,128)S(1)}, f32[256,768]{1,0:T(8,128)S(1)}, u32[]{:S(2)}, u32[]{:S(2)}) collective-permute-start(f32[256,768]{1,0:T(8,128)S(1)} %get-tuple-element.410.refs_0_), channel_id=1, source_target_pairs={{0,8},{4,12},{24,16},{28,20},{1,9},{5,13},{25,17},{29,21},{2,10},{... | collective-permute-start | bytes 2359304 | tf_op jit(solution)/shard_map/ppermute | solution.py:39
  97.0 6.8 %collective-permute-done.59.refs_1_ = f32[256,768]{1,0:T(8,128)S(1)} collective-permute-done((f32[256,768]{1,0:T(8,128)S(1)}, f32[256,768]{1,0:T(8,128)S(1)}, u32[]{:S(2)}, u32[]{:S(2)}) %collective-permute-start.59) | collective-permute-done | bytes 786464 | tf_op jit(solution)/shard_map/ppermute | solution.py:31
  106.1 3.1 %collective-permute-done.58.refs_1_ = f32[192,768]{1,0:T(8,128)S(1)} collective-permute-done((f32[192,768]{1,0:T(8,128)S(1)}, f32[192,768]{1,0:T(8,128)S(1)}, u32[]{:S(2)}, u32[]{:S(2)}) %collective-permute-start.58) | collective-permute-done | bytes 589856 | tf_op jit(solution)/shard_map/ppermute | solution.py:35
  109.3 3.1 %collective-permute-start.64 = (f32[192,768]{1,0:T(8,128)S(1)}, f32[192,768]{1,0:T(8,128)S(1)}, u32[]{:S(2)}, u32[]{:S(2)}) collective-permute-start(f32[192,768]{1,0:T(8,128)S(1)} %get-tuple-element.406.refs_0_), channel_id=1, source_target_pairs={{0,8},{4,12},{24,16},{28,20},{1,9},{5,13},{25,17},{29,21},{2,10},{... | collective-permute-start | bytes 1769480 | tf_op jit(solution)/shard_map/ppermute | solution.py:39
  116.3 5.4 %collective-permute-done.65.refs_1_ = f32[200,768]{1,0:T(8,128)S(1)} collective-permute-done((f32[200,768]{1,0:T(8,128)S(1)}, f32[200,768]{1,0:T(8,128)S(1)}, u32[]{:S(2)}, u32[]{:S(2)}) %collective-permute-start.65) | collective-permute-done | bytes 614432 | tf_op jit(solution)/shard_map/ppermute | solution.py:35
  121.7 3.7 %collective-permute-start.71 = (f32[200,768]{1,0:T(8,128)S(1)}, f32[200,768]{1,0:T(8,128)S(1)}, u32[]{:S(2)}, u32[]{:S(2)}) collective-permute-start(f32[200,768]{1,0:T(8,128)S(1)} %get-tuple-element.420.refs_0_), channel_id=1, source_target_pairs={{0,8},{4,12},{24,16},{28,20},{1,9},{5,13},{25,17},{29,21},{2,10},{... | collective-permute-start | bytes 1843208 | tf_op jit(solution)/shard_map/ppermute | solution.py:39
  127.1 3.7 %collective-permute-done.63.refs_1_ = f32[256,768]{1,0:T(8,128)S(1)} collective-permute-done((f32[256,768]{1,0:T(8,128)S(1)}, f32[256,768]{1,0:T(8,128)S(1)}, u32[]{:S(2)}, u32[]{:S(2)}) %collective-permute-start.63) | collective-permute-done | bytes 786464 | tf_op jit(solution)/shard_map/ppermute | solution.py:31
  135.2 3.0 %collective-permute-start.83 = (f32[256,768]{1,0:T(8,128)S(1)}, f32[256,768]{1,0:T(8,128)S(1)}, u32[]{:S(2)}, u32[]{:S(2)}) collective-permute-start(f32[256,768]{1,0:T(8,128)S(1)} %get-tuple-element.443.refs_0_), channel_id=1, source_target_pairs={{0,4},{4,0},{24,28},{28,24},{1,5},{5,1},{25,29},{29,25},{2,6},{6,2... | collective-permute-start | bytes 2359304 | tf_op jit(solution)/shard_map/ppermute | solution.py:39
  138.9 4.0 %collective-permute-start.78 = (f32[128,768]{1,0:T(8,128)S(1)}, f32[128,768]{1,0:T(8,128)S(1)}, u32[]{:S(2)}, u32[]{:S(2)}) collective-permute-start(f32[128,768]{1,0:T(8,128)S(1)} %get-tuple-element.433.refs_0_), channel_id=1, source_target_pairs={{0,8},{4,12},{24,16},{28,20},{1,9},{5,13},{25,17},{29,21},{2,10},{... | collective-permute-start | bytes 1179656 | tf_op jit(solution)/shard_map/ppermute | solution.py:39
  145.1 3.6 %collective-permute-done.78.refs_1_ = f32[128,768]{1,0:T(8,128)S(1)} collective-permute-done((f32[128,768]{1,0:T(8,128)S(1)}, f32[128,768]{1,0:T(8,128)S(1)}, u32[]{:S(2)}, u32[]{:S(2)}) %collective-permute-start.78) | collective-permute-done | bytes 393248 | tf_op jit(solution)/shard_map/ppermute | solution.py:39
  148.8 5.4 %collective-permute-done.77.refs_1_ = f32[256,768]{1,0:T(8,128)S(1)} collective-permute-done((f32[256,768]{1,0:T(8,128)S(1)}, f32[256,768]{1,0:T(8,128)S(1)}, u32[]{:S(2)}, u32[]{:S(2)}) %collective-permute-start.77) | collective-permute-done | bytes 786464 | tf_op jit(solution)/shard_map/ppermute | solution.py:39
  158.5 8.2 %collective-permute-done.75.refs_1_ = f32[192,768]{1,0:T(8,128)S(1)} collective-permute-done((f32[192,768]{1,0:T(8,128)S(1)}, f32[192,768]{1,0:T(8,128)S(1)}, u32[]{:S(2)}, u32[]{:S(2)}) %collective-permute-start.75) | collective-permute-done | bytes 589856 | tf_op jit(solution)/shard_map/ppermute | solution.py:39
  169.4 5.4 %collective-permute-done.85.refs_1_ = f32[256,768]{1,0:T(8,128)S(1)} collective-permute-done((f32[256,768]{1,0:T(8,128)S(1)}, f32[256,768]{1,0:T(8,128)S(1)}, u32[]{:S(2)}, u32[]{:S(2)}) %collective-permute-start.85) | collective-permute-done | bytes 786464 | tf_op jit(solution)/shard_map/ppermute | solution.py:35
  182.1 5.1 %collective-permute-done.90.refs_1_ = f32[128,768]{1,0:T(8,128)S(1)} collective-permute-done((f32[128,768]{1,0:T(8,128)S(1)}, f32[128,768]{1,0:T(8,128)S(1)}, u32[]{:S(2)}, u32[]{:S(2)}) %collective-permute-start.90) | collective-permute-done | bytes 393248 | tf_op jit(solution)/shard_map/ppermute | solution.py:39
  191.2 6.0 %collective-permute-done.88.refs_1_ = f32[200,768]{1,0:T(8,128)S(1)} collective-permute-done((f32[200,768]{1,0:T(8,128)S(1)}, f32[200,768]{1,0:T(8,128)S(1)}, u32[]{:S(2)}, u32[]{:S(2)}) %collective-permute-start.88) | collective-permute-done | bytes 614432 | tf_op jit(solution)/shard_map/ppermute | solution.py:35
  198.4 4.8 %collective-permute-done.82.refs_3_ = f32[128,768]{1,0:T(8,128)S(1)} collective-permute-done((f32[128,768]{1,0:T(8,128)S(1)}, f32[128,768]{1,0:T(8,128)S(1)}, u32[]{:S(2)}, u32[]{:S(2)}) %collective-permute-start.82) | collective-permute-done | bytes 393248 | tf_op jit(solution)/shard_map/ppermute | solution.py:39
  (258 shorter events, 85.0 us)
Async XLA Ops:
  15.1 13.6 %collective-permute-start.8 = (f32[128,768]{1,0:T(8,128)S(1)}, f32[128,768]{1,0:T(8,128)S(1)}, u32[]{:S(2)}, u32[]{:S(2)}) collective-permute-start(f32[128,768]{1,0:T(8,128)S(1)} %get-tuple-element.265.refs_0_), channel_id=1, source_target_pairs={{0,2},{1,3},{2,0},{3,1},{4,6},{5,7},{6,4},{7,5},{8,10},{9,11},{10,... | collective-permute-start | bytes 1179656 | tf_op jit(solution)/shard_map/ppermute | solution.py:31
  52.0 20.5 %collective-permute-start.50 = (f32[256,768]{1,0:T(8,128)S(1)}, f32[256,768]{1,0:T(8,128)S(1)}, u32[]{:S(2)}, u32[]{:S(2)}) collective-permute-start(f32[256,768]{1,0:T(8,128)S(1)} %get-tuple-element.356), channel_id=1, source_target_pairs={{0,4},{4,0},{8,12},{12,8},{16,20},{20,16},{24,28},{28,24},{1,5},{5... | collective-permute-start | bytes 2359304 | tf_op jit(solution)/shard_map/ppermute | solution.py:35
  53.9 22.8 %collective-permute-start.55 = (f32[2,128,768]{2,1,0:T(8,128)S(1)}, f32[2,128,768]{2,1,0:T(8,128)S(1)}, u32[]{:S(2)}, u32[]{:S(2)}) collective-permute-start(f32[2,128,768]{2,1,0:T(8,128)S(1)} %get-tuple-element.363.refs_0_), channel_id=1, source_target_pairs={{0,8},{4,12},{24,16},{28,20},{1,9},{5,13},{25,17},{29,21},{2,10},{... | collective-permute-start | bytes 2359304 | tf_op jit(solution)/shard_map/ppermute | solution.py:39
  64.9 19.1 %collective-permute-start.57 = (f32[256,768]{1,0:T(8,128)S(1)}, f32[256,768]{1,0:T(8,128)S(1)}, u32[]{:S(2)}, u32[]{:S(2)}) collective-permute-start(f32[256,768]{1,0:T(8,128)S(1)} %get-tuple-element.374), channel_id=1, source_target_pairs={{0,1},{1,0},{2,3},{3,2},{4,5},{5,4},{6,7},{7,6},{8,9},{9,8},{10,11... | collective-permute-start | bytes 2359304 | tf_op jit(solution)/shard_map/ppermute | solution.py:27
  67.2 21.0 %collective-permute-start.62 = (f32[256,768]{1,0:T(8,128)S(1)}, f32[256,768]{1,0:T(8,128)S(1)}, u32[]{:S(2)}, u32[]{:S(2)}) collective-permute-start(f32[256,768]{1,0:T(8,128)S(1)} %get-tuple-element.396), channel_id=1, source_target_pairs={{0,4},{4,0},{8,12},{12,8},{16,20},{20,16},{24,28},{28,24},{1,5},{5... | collective-permute-start | bytes 2359304 | tf_op jit(solution)/shard_map/ppermute | solution.py:35
  72.6 22.0 %collective-permute-start.60 = (f32[256,768]{1,0:T(8,128)S(1)}, f32[256,768]{1,0:T(8,128)S(1)}, u32[]{:S(2)}, u32[]{:S(2)}) collective-permute-start(f32[256,768]{1,0:T(8,128)S(1)} %get-tuple-element.392.refs_0_), channel_id=1, source_target_pairs={{0,8},{4,12},{24,16},{28,20},{1,9},{5,13},{25,17},{29,21},{2,10},{... | collective-permute-start | bytes 2359304 | tf_op jit(solution)/shard_map/ppermute | solution.py:39
  78.2 14.7 %collective-permute-start.61 = (f32[128,768]{1,0:T(8,128)S(1)}, f32[128,768]{1,0:T(8,128)S(1)}, u32[]{:S(2)}, u32[]{:S(2)}) collective-permute-start(f32[128,768]{1,0:T(8,128)S(1)} %get-tuple-element.394), channel_id=1, source_target_pairs={{8,16},{12,20},{16,8},{20,12},{9,17},{13,21},{17,9},{21,13},{10,18... | collective-permute-start | bytes 1179656 | tf_op jit(solution)/shard_map/ppermute | solution.py:39
  84.0 19.8 %collective-permute-start.59 = (f32[256,768]{1,0:T(8,128)S(1)}, f32[256,768]{1,0:T(8,128)S(1)}, u32[]{:S(2)}, u32[]{:S(2)}) collective-permute-start(f32[256,768]{1,0:T(8,128)S(1)} %get-tuple-element.379.refs_0_), channel_id=1, source_target_pairs={{0,2},{1,3},{2,0},{3,1},{4,6},{5,7},{6,4},{7,5},{8,10},{9,11},{10,... | collective-permute-start | bytes 2359304 | tf_op jit(solution)/shard_map/ppermute | solution.py:31
  85.9 26.5 %collective-permute-start.56 = (f32[256,768]{1,0:T(8,128)S(1)}, f32[256,768]{1,0:T(8,128)S(1)}, u32[]{:S(2)}, u32[]{:S(2)}) collective-permute-start(f32[256,768]{1,0:T(8,128)S(1)} %get-tuple-element.368), channel_id=1, source_target_pairs={{0,1},{1,0},{2,3},{3,2},{4,5},{5,4},{6,7},{7,6},{8,9},{9,8},{10,11... | collective-permute-start | bytes 2359304 | tf_op jit(solution)/shard_map/ppermute | solution.py:27
  88.2 25.8 %collective-permute-start.67 = (f32[256,768]{1,0:T(8,128)S(1)}, f32[256,768]{1,0:T(8,128)S(1)}, u32[]{:S(2)}, u32[]{:S(2)}) collective-permute-start(f32[256,768]{1,0:T(8,128)S(1)} %get-tuple-element.410.refs_0_), channel_id=1, source_target_pairs={{0,8},{4,12},{24,16},{28,20},{1,9},{5,13},{25,17},{29,21},{2,10},{... | collective-permute-start | bytes 2359304 | tf_op jit(solution)/shard_map/ppermute | solution.py:39
  93.0 16.2 %collective-permute-start.58 = (f32[192,768]{1,0:T(8,128)S(1)}, f32[192,768]{1,0:T(8,128)S(1)}, u32[]{:S(2)}, u32[]{:S(2)}) collective-permute-start(f32[192,768]{1,0:T(8,128)S(1)} %get-tuple-element.378), channel_id=1, source_target_pairs={{0,4},{4,0},{8,12},{12,8},{16,20},{20,16},{24,28},{28,24},{1,5},{5... | collective-permute-start | bytes 1769480 | tf_op jit(solution)/shard_map/ppermute | solution.py:35
  94.7 20.2 %collective-permute-start.66 = (f32[256,768]{1,0:T(8,128)S(1)}, f32[256,768]{1,0:T(8,128)S(1)}, u32[]{:S(2)}, u32[]{:S(2)}) collective-permute-start(f32[256,768]{1,0:T(8,128)S(1)} %get-tuple-element.409.refs_0_), channel_id=1, source_target_pairs={{8,16},{12,20},{16,8},{20,12},{9,17},{13,21},{17,9},{21,13},{10,18... | collective-permute-start | bytes 2359304 | tf_op jit(solution)/shard_map/ppermute | solution.py:39
  103.9 17.8 %collective-permute-start.65 = (f32[200,768]{1,0:T(8,128)S(1)}, f32[200,768]{1,0:T(8,128)S(1)}, u32[]{:S(2)}, u32[]{:S(2)}) collective-permute-start(f32[200,768]{1,0:T(8,128)S(1)} %get-tuple-element.408), channel_id=1, source_target_pairs={{0,4},{4,0},{8,12},{12,8},{16,20},{20,16},{24,28},{28,24},{1,5},{5... | collective-permute-start | bytes 1843208 | tf_op jit(solution)/shard_map/ppermute | solution.py:35
  109.3 16.1 %collective-permute-start.64 = (f32[192,768]{1,0:T(8,128)S(1)}, f32[192,768]{1,0:T(8,128)S(1)}, u32[]{:S(2)}, u32[]{:S(2)}) collective-permute-start(f32[192,768]{1,0:T(8,128)S(1)} %get-tuple-element.406.refs_0_), channel_id=1, source_target_pairs={{0,8},{4,12},{24,16},{28,20},{1,9},{5,13},{25,17},{29,21},{2,10},{... | collective-permute-start | bytes 1769480 | tf_op jit(solution)/shard_map/ppermute | solution.py:39
  112.5 18.3 %collective-permute-start.63 = (f32[256,768]{1,0:T(8,128)S(1)}, f32[256,768]{1,0:T(8,128)S(1)}, u32[]{:S(2)}, u32[]{:S(2)}) collective-permute-start(f32[256,768]{1,0:T(8,128)S(1)} %get-tuple-element.405.refs_0_), channel_id=1, source_target_pairs={{0,2},{1,3},{2,0},{3,1},{4,6},{5,7},{6,4},{7,5},{8,10},{9,11},{10,... | collective-permute-start | bytes 2359304 | tf_op jit(solution)/shard_map/ppermute | solution.py:31
  114.1 17.4 %collective-permute-start.74 = (f32[256,768]{1,0:T(8,128)S(1)}, f32[256,768]{1,0:T(8,128)S(1)}, u32[]{:S(2)}, u32[]{:S(2)}) collective-permute-start(f32[256,768]{1,0:T(8,128)S(1)} %get-tuple-element.424.refs_0_), channel_id=1, source_target_pairs={{8,16},{12,20},{16,8},{20,12},{9,17},{13,21},{17,9},{21,13},{10,18... | collective-permute-start | bytes 2359304 | tf_op jit(solution)/shard_map/ppermute | solution.py:39
  115.0 20.2 %collective-permute-start.72 = (f32[256,768]{1,0:T(8,128)S(1)}, f32[256,768]{1,0:T(8,128)S(1)}, u32[]{:S(2)}, u32[]{:S(2)}) collective-permute-start(f32[256,768]{1,0:T(8,128)S(1)} %get-tuple-element.421.refs_0_), channel_id=1, source_target_pairs={{8,0},{12,4},{16,24},{20,28},{9,1},{13,5},{17,25},{21,29},{10,2},{... | collective-permute-start | bytes 2359304 | tf_op jit(solution)/shard_map/ppermute | solution.py:39
  121.7 17.2 %collective-permute-start.71 = (f32[200,768]{1,0:T(8,128)S(1)}, f32[200,768]{1,0:T(8,128)S(1)}, u32[]{:S(2)}, u32[]{:S(2)}) collective-permute-start(f32[200,768]{1,0:T(8,128)S(1)} %get-tuple-element.420.refs_0_), channel_id=1, source_target_pairs={{0,8},{4,12},{24,16},{28,20},{1,9},{5,13},{25,17},{29,21},{2,10},{... | collective-permute-start | bytes 1843208 | tf_op jit(solution)/shard_map/ppermute | solution.py:39
  131.7 22.5 %collective-permute-start.77 = (f32[256,768]{1,0:T(8,128)S(1)}, f32[256,768]{1,0:T(8,128)S(1)}, u32[]{:S(2)}, u32[]{:S(2)}) collective-permute-start(f32[256,768]{1,0:T(8,128)S(1)} %get-tuple-element.432.refs_0_), channel_id=1, source_target_pairs={{8,0},{12,4},{16,24},{20,28},{9,1},{13,5},{17,25},{21,29},{10,2},{... | collective-permute-start | bytes 2359304 | tf_op jit(solution)/shard_map/ppermute | solution.py:39
  135.2 20.4 %collective-permute-start.83 = (f32[256,768]{1,0:T(8,128)S(1)}, f32[256,768]{1,0:T(8,128)S(1)}, u32[]{:S(2)}, u32[]{:S(2)}) collective-permute-start(f32[256,768]{1,0:T(8,128)S(1)} %get-tuple-element.443.refs_0_), channel_id=1, source_target_pairs={{0,4},{4,0},{24,28},{28,24},{1,5},{5,1},{25,29},{29,25},{2,6},{6,2... | collective-permute-start | bytes 2359304 | tf_op jit(solution)/shard_map/ppermute | solution.py:39
  143.0 14.1 %collective-permute-start.76 = (f32[200,768]{1,0:T(8,128)S(1)}, f32[200,768]{1,0:T(8,128)S(1)}, u32[]{:S(2)}, u32[]{:S(2)}) collective-permute-start(f32[200,768]{1,0:T(8,128)S(1)} %get-tuple-element.431.refs_0_), channel_id=1, source_target_pairs={{8,16},{12,20},{16,8},{20,12},{9,17},{13,21},{17,9},{21,13},{10,18... | collective-permute-start | bytes 1843208 | tf_op jit(solution)/shard_map/ppermute | solution.py:39
  143.8 22.8 %collective-permute-start.75 = (f32[192,768]{1,0:T(8,128)S(1)}, f32[192,768]{1,0:T(8,128)S(1)}, u32[]{:S(2)}, u32[]{:S(2)}) collective-permute-start(f32[192,768]{1,0:T(8,128)S(1)} %get-tuple-element.430.refs_0_), channel_id=1, source_target_pairs={{8,0},{12,4},{16,24},{20,28},{9,1},{13,5},{17,25},{21,29},{10,2},{... | collective-permute-start | bytes 1769480 | tf_op jit(solution)/shard_map/ppermute | solution.py:39
  148.7 18.7 %collective-permute-start.69 = (f32[256,768]{1,0:T(8,128)S(1)}, f32[256,768]{1,0:T(8,128)S(1)}, u32[]{:S(2)}, u32[]{:S(2)}) collective-permute-start(f32[256,768]{1,0:T(8,128)S(1)} %get-tuple-element.418.refs_1_), channel_id=1, source_target_pairs={{0,1},{1,0},{2,3},{3,2},{4,5},{5,4},{6,7},{7,6},{8,9},{9,8},{10,11... | collective-permute-start | bytes 2359304 | tf_op jit(solution)/shard_map/ppermute | solution.py:27
  154.3 20.5 %collective-permute-start.85 = (f32[256,768]{1,0:T(8,128)S(1)}, f32[256,768]{1,0:T(8,128)S(1)}, u32[]{:S(2)}, u32[]{:S(2)}) collective-permute-start(f32[256,768]{1,0:T(8,128)S(1)} %get-tuple-element.444.refs_0_), channel_id=1, source_target_pairs={{0,4},{4,0},{8,12},{12,8},{16,20},{20,16},{24,28},{28,24},{1,5},{5... | collective-permute-start | bytes 2359304 | tf_op jit(solution)/shard_map/ppermute | solution.py:35
  155.6 22.4 %collective-permute-start.84 = (f32[256,768]{1,0:T(8,128)S(1)}, f32[256,768]{1,0:T(8,128)S(1)}, u32[]{:S(2)}, u32[]{:S(2)}) collective-permute-start(f32[256,768]{1,0:T(8,128)S(1)} %collective-permute-done.83.refs_1_), channel_id=1, source_target_pairs={{0,8},{4,12},{24,16},{28,20},{1,9},{5,13},{25,17},{29,21},{2,10},{... | collective-permute-start | bytes 2359304 | tf_op jit(solution)/shard_map/ppermute | solution.py:39
  157.2 22.1 %collective-permute-start.87 = (f32[200,768]{1,0:T(8,128)S(1)}, f32[200,768]{1,0:T(8,128)S(1)}, u32[]{:S(2)}, u32[]{:S(2)}) collective-permute-start(f32[200,768]{1,0:T(8,128)S(1)} %get-tuple-element.453.refs_0_), channel_id=1, source_target_pairs={{8,0},{12,4},{16,24},{20,28},{9,1},{13,5},{17,25},{21,29},{10,2},{... | collective-permute-start | bytes 1843208 | tf_op jit(solution)/shard_map/ppermute | solution.py:39
  167.4 21.1 %collective-permute-start.89 = (f32[192,768]{1,0:T(8,128)S(1)}, f32[192,768]{1,0:T(8,128)S(1)}, u32[]{:S(2)}, u32[]{:S(2)}) collective-permute-start(f32[192,768]{1,0:T(8,128)S(1)} %get-tuple-element.456.refs_0_), channel_id=1, source_target_pairs={{0,4},{4,0},{8,12},{12,8},{16,20},{20,16},{24,28},{28,24},{1,5},{5... | collective-permute-start | bytes 1769480 | tf_op jit(solution)/shard_map/ppermute | solution.py:35
  178.0 26.1 %collective-permute-start.68 = (f32[256,768]{1,0:T(8,128)S(1)}, f32[256,768]{1,0:T(8,128)S(1)}, u32[]{:S(2)}, u32[]{:S(2)}) collective-permute-start(f32[256,768]{1,0:T(8,128)S(1)} %get-tuple-element.416.refs_1_), channel_id=1, source_target_pairs={{0,1},{1,0},{2,3},{3,2},{4,5},{5,4},{6,7},{7,6},{8,9},{9,8},{10,11... | collective-permute-start | bytes 2359304 | tf_op jit(solution)/shard_map/ppermute | solution.py:27
  179.4 17.8 %collective-permute-start.88 = (f32[200,768]{1,0:T(8,128)S(1)}, f32[200,768]{1,0:T(8,128)S(1)}, u32[]{:S(2)}, u32[]{:S(2)}) collective-permute-start(f32[200,768]{1,0:T(8,128)S(1)} %get-tuple-element.455.refs_0_), channel_id=1, source_target_pairs={{0,4},{4,0},{8,12},{12,8},{16,20},{20,16},{24,28},{28,24},{1,5},{5... | collective-permute-start | bytes 1843208 | tf_op jit(solution)/shard_map/ppermute | solution.py:35
  180.8 17.6 %collective-permute-start.81 = (f32[128,768]{1,0:T(8,128)S(1)}, f32[128,768]{1,0:T(8,128)S(1)}, u32[]{:S(2)}, u32[]{:S(2)}) collective-permute-start(f32[128,768]{1,0:T(8,128)S(1)} %get-tuple-element.442.refs_0_), channel_id=1, source_target_pairs={{8,0},{12,4},{16,24},{20,28},{9,1},{13,5},{17,25},{21,29},{10,2},{... | collective-permute-start | bytes 1179656 | tf_op jit(solution)/shard_map/ppermute | solution.py:39
  187.2 16.1 %collective-permute-start.82 = (f32[128,768]{1,0:T(8,128)S(1)}, f32[128,768]{1,0:T(8,128)S(1)}, u32[]{:S(2)}, u32[]{:S(2)}) collective-permute-start(f32[128,768]{1,0:T(8,128)S(1)} %collective-permute-done.80.refs_1_), channel_id=1, source_target_pairs={{8,0},{12,4},{16,24},{20,28},{9,1},{13,5},{17,25},{21,29},{10,2},{... | collective-permute-start | bytes 1179656 | tf_op jit(solution)/shard_map/ppermute | solution.py:39
  188.5 16.9 %collective-permute-start.91 = (f32[128,768]{1,0:T(8,128)S(1)}, f32[128,768]{1,0:T(8,128)S(1)}, u32[]{:S(2)}, u32[]{:S(2)}) collective-permute-start(f32[128,768]{1,0:T(8,128)S(1)} %get-tuple-element.474.refs_0_), channel_id=1, source_target_pairs={{0,4},{4,0},{8,12},{12,8},{16,20},{20,16},{24,28},{28,24},{1,5},{5... | collective-permute-start | bytes 1179656 | tf_op jit(solution)/shard_map/ppermute | solution.py:35
  (82 other events, 345.9 us)
